TPU v7x, 512 devices: a whole 4x4x16 slice. The times are simulated.
512 devices in a mesh: dp: 32 (over z, x_hi), replica: 16 (over y, x_lo, core).
Axes of the slice: x: 4 (x_hi: 2, x_lo: 2; x = x_hi * 2 + x_lo), y: 4, z: 16, core: 2. Of those that a mesh axis runs over, the one named last changes fastest.
Arguments:
- grad_parts: bfloat16 [1024, 256, 512], P('dp', 'replica'), may hold values from -1.1953125 to 1.1953125
- master_weight: float32 [8192, 512], P(('dp', 'replica')), may hold values from -0.0625 to 0.0625
- moment_one: float32 [8192, 512], P(('dp', 'replica')), may hold values from -1.8 to 1.8
- moment_two: float32 [8192, 512], P(('dp', 'replica')), may hold values from 0.05 to 2
- queries: bfloat16 [16, 4096, 4096], P('replica', 'dp'), may hold values from -5 to 5
- keys_in: bfloat16 [16, 4096, 512], P('replica', 'dp'), may hold values from -5 to 5
- hidden: bfloat16 [16, 4096, 8192], P('replica', 'dp'), may hold values from -6 to 6
- segment_ids: int32 [16, 4096], P('replica', 'dp'), may hold values from 0 to 20, never falling along the last dimension, each value on 1 to 384 neighbouring positions
- packed_len: int32 [16], P('replica'), may hold values from 2048 to 4096
Outputs:
- new_master: float32 [8192, 512], P(('dp', 'replica'))
- new_first: float32 [8192, 512], P(('dp', 'replica'))
- new_second: float32 [8192, 512], P(('dp', 'replica'))
- attended: bfloat16 [16, 4096, 4096], P('replica', 'dp')
Inputs may be any that keep to these rules, and one draw needn't show every extreme that they name: `segment_ids`: on each replica the numbers never fall along positions, and each prompt covers at most 384 positions, one exactly that many.
All inputs are finite; a program needn't handle non-finite values.
Results may differ from a plain program's by a relative error of at most 0.009.
Values may be sent and summed in bfloat16 or wider, within the bound.
A program may use at most 64 MiB of HBM per device.

v0:
```python
import jax
import jax.numpy as jnp
from jax import lax
from jax.sharding import PartitionSpec as P

HD = 128


beta_one = 0.9
beta_two = 0.95
bias_one = 1.0 - 0.9**10
bias_two = 1.0 - 0.95**10
adam_eps = 1e-08
learn_rate = 0.002
weight_decay = 0.1


def passed_along(block, axis, distance):
    devices = range(lax.axis_size(axis))
    route = [(i - distance, i) for i in devices if i - distance in devices]
    return lax.ppermute(block, axis, route)


def adam_update(grad_sum, master, moment_first, moment_second):
    first_new = beta_one * moment_first + (1.0 - beta_one) * grad_sum
    second_new = beta_two * moment_second + (1.0 - beta_two) * grad_sum * grad_sum
    step_dir = (
        first_new / bias_one / (jnp.sqrt(second_new / bias_two) + adam_eps) + weight_decay * master
    )
    master_new = master - learn_rate * step_dir
    return (master_new, first_new, second_new, master_new.astype(jnp.bfloat16))


def prefill(queries, keys_in, value_states, segment_ids, packed_len):
    local_len = queries.shape[1]
    heads_kv = keys_in.shape[2] // HD
    groups = queries.shape[2] // keys_in.shape[2]
    device_pos = lax.axis_index("dp")
    seg_here = segment_ids[0].astype(jnp.bfloat16)
    steps_back = jnp.arange(local_len, dtype=jnp.int32)
    key_list = []
    value_list = []
    seg_list = []
    valid_list = []
    pos_list = []
    for offset in (3, 2, 1):
        moved_keys, moved_values, moved_segs = passed_along(
            (keys_in[0], value_states, seg_here), "dp", offset
        )
        key_list.append(moved_keys)
        value_list.append(moved_values)
        seg_list.append(moved_segs)
        valid_list.append(jnp.broadcast_to(device_pos >= offset, (local_len,)))
        pos_list.append((device_pos - offset) * local_len + steps_back)
    key_list.append(keys_in[0])
    value_list.append(value_states)
    seg_list.append(seg_here)
    valid_list.append(jnp.ones((local_len,), jnp.bool_))
    query_pos = device_pos * local_len + steps_back
    pos_list.append(query_pos)
    all_keys = jnp.concatenate(key_list, axis=0).reshape(4 * local_len, heads_kv, HD)
    all_values = jnp.concatenate(value_list, axis=0).reshape(4 * local_len, heads_kv, HD)
    seg_keys = jnp.concatenate(seg_list, axis=0)
    key_valid = jnp.concatenate(valid_list, axis=0)
    key_pos = jnp.concatenate(pos_list, axis=0)
    allowed = (
        (seg_here[:, None] == seg_keys[None, :])
        & (key_pos[None, :] <= query_pos[:, None])
        & key_valid[None, :]
    )
    query_heads = queries[0].reshape(local_len, heads_kv, groups, HD)
    scores = jnp.einsum(
        "qhgd,khd->hgqk", query_heads, all_keys, preferred_element_type=jnp.float32
    ) * HD ** (-0.5)
    scores = jnp.where(allowed, scores, -jnp.inf)
    row_max = jnp.max(scores, axis=-1, keepdims=True)
    weights = jnp.where(allowed, jnp.exp(scores - row_max), 0.0)
    totals = jnp.sum(weights, axis=-1, keepdims=True)
    rounded = weights.astype(jnp.bfloat16)
    mixed_out = jnp.einsum(
        "hgqk,khd->qhgd", rounded, all_values, preferred_element_type=jnp.float32
    )
    mixed_out = mixed_out / jnp.transpose(totals, (2, 0, 1, 3))
    mixed_out = mixed_out.reshape(local_len, heads_kv * groups * HD)
    query_live = query_pos < packed_len[0]
    return jnp.where(query_live[:, None], mixed_out, 0.0).astype(jnp.bfloat16)[None]


def on_device(
    grad_parts,
    master_weight,
    moment_one,
    moment_two,
    queries,
    keys_in,
    hidden,
    segment_ids,
    packed_len,
):
    grad_terms = grad_parts.astype(jnp.float32)
    grad_sum = lax.psum_scatter(
        grad_terms.astype(jnp.bfloat16), "dp", scatter_dimension=0, tiled=True
    ).astype(jnp.float32)[0]
    new_master, new_first, new_second, rounded_rows = adam_update(
        grad_sum, master_weight, moment_one, moment_two
    )
    hidden_rows = hidden[0]
    group_rows = lax.all_gather(rounded_rows, "replica", axis=0, tiled=True)
    projected = jnp.dot(
        hidden_rows,
        lax.all_gather(group_rows, "dp", axis=0, tiled=True),
        preferred_element_type=jnp.float32,
    )
    value_states = projected.astype(jnp.bfloat16)
    attended = prefill(queries, keys_in, value_states, segment_ids, packed_len)
    return (new_master, new_first, new_second, attended)


def solution(mesh):
    in_specs = (
        P("dp", "replica", None),
        P(("dp", "replica"), None),
        P(("dp", "replica"), None),
        P(("dp", "replica"), None),
        P("replica", "dp", None),
        P("replica", "dp", None),
        P("replica", "dp", None),
        P("replica", "dp"),
        P("replica"),
    )
    out_specs = (
        P(("dp", "replica"), None),
        P(("dp", "replica"), None),
        P(("dp", "replica"), None),
        P("replica", "dp", None),
    )
    return jax.shard_map(
        on_device, mesh=mesh, in_specs=in_specs, out_specs=out_specs, check_vma=False
    )
```

profile of v0, /device:TPU:1, one launch (start us, length us, event | category | flops | bytes accessed | tf_op | source)
XLA Modules:
  0.0 894.5 jit_solution(11459201803201772713)
XLA Ops:
  7.2 0.0 copy-start
  7.2 0.0 reduce-scatter.2.cloned.1.call-start
  7.2 0.7 reduce-scatter.2.cloned.1.call-update
  7.9 0.0 all-gather.2.cloned.1.call-start
  8.0 636.2 %reduce-scatter.2.cloned.1.call-done = bf16[1,16,512]{2,1,0:T(8,128)(2,1)} async-done(((bf16[32,16,512]{2,1,0:T(8,128)(2,1)}), bf16[1,16,512]{2,1,0:T(8,128)(2,1)}) %reduce-scatter.2.cloned.1.call-update) | async-done | bytes 16400 | tf_op jit(solution)/shard_map/reduce_scatter | solution.py:101
  644.1 1.5 fusion.30
  645.6 32.3 %all_gather.6 = bf16[256,512]{1,0:T(8,128)(2,1)} all-gather(bf16[16,512]{1,0:T(8,128)(2,1)S(1)} %get-tuple-element.4), channel_id=1, replica_groups=mesh['dp'=32,'replica'=16] {'replica'}, dimensions={0}, use_global_device_ids=true | all-gather | bytes 278528 | tf_op jit(solution)/shard_map/all_gather | solution.py:108
  677.9 0.0 all-gather.2.cloned.1.call-update
  677.9 0.7 convert_bitcast_fusion
  678.6 5.0 collective-permute-start.3
  683.6 3.7 collective-permute-start.4
  687.3 3.6 collective-permute-start.5
  690.9 1.7 copy.17
  692.6 4.1 collective-permute-start.6
  696.7 3.4 collective-permute-start.7
  700.8 0.6 broadcast_compare_fusion
  701.5 1.0 copy.22
  702.5 1.4 copy.31
  703.9 0.0 collective-permute-done.3
  704.0 4.7 collective-permute-start.8
  708.6 0.0 collective-permute-done.4
  708.6 0.0 collective-permute-done.5
  708.6 0.7 pad_maximum_fusion.1
  709.3 0.9 and_and_fusion
  710.2 0.0 collective-permute-done.6
  710.2 0.6 copy-done.3
  710.9 1.0 copy.19
  711.9 0.0 collective-permute-done.7
  711.9 0.6 copy-done.2
  712.6 1.0 copy.20
  713.6 0.0 collective-permute-done.8
  713.6 1.7 copy.21
  715.3 5.4 fusion.17
  720.7 139.6 %all-gather.2.cloned.1.call-done = bf16[8192,512]{1,0:T(8,128)(2,1)} async-done(((bf16[256,512]{1,0:T(8,128)(2,1)}), bf16[8192,512]{1,0:T(8,128)(2,1)}) %all-gather.2.cloned.1.call-update) | async-done | bytes 8388624 | tf_op jit(solution)/shard_map/all_gather | solution.py:111
  860.3 4.8 fusion.14
  865.1 2.3 collective-permute-start
  867.4 2.4 collective-permute-start.1
  869.8 5.0 collective-permute-start.2
  874.9 5.8 fusion.33
  880.7 0.0 collective-permute-done
  880.7 0.0 collective-permute-done.1
  880.7 0.0 collective-permute-done.2
  880.8 0.2 copy.30
  881.0 0.0 copy-start.5
  881.0 3.9 bitcast_divide_fusion
  884.9 1.5 copy.26
  886.4 0.0 copy-done.5
  886.4 1.2 select_convert_fusion
  (17 shorter events, 0.1 us)
Async XLA Ops:
  7.2 853.1 %copy-start = (bf16[1,128,8192]{2,1,0:T(8,128)(2,1)S(1)}, bf16[1,128,8192]{2,1,0:T(8,128)(2,1)}, u32[]{:S(2)}) copy-start(bf16[1,128,8192]{2,1,0:T(8,128)(2,1)} %param.15) | copy-start | bytes 6291460
  7.2 637.0 %reduce-scatter.2.cloned.1.call-start = ((), (), s32[]{:S(2)}) async-start(), calls=%async_computation.1 | async-start | bytes 540672 | tf_op jit(solution)/shard_map/reduce_scatter | solution.py:101
  7.9 852.4 %all-gather.2.cloned.1.call-start = ((), (), s32[]{:S(2)}) async-start(), calls=%async_computation.2 | async-start | bytes 8650752 | tf_op jit(solution)/shard_map/all_gather | solution.py:111
  678.6 25.3 %collective-permute-start.3 = (bf16[128]{0:T(256)(128)(2,1)S(1)}, bf16[128]{0:T(256)(128)(2,1)}, u32[]{:S(2)}, u32[]{:S(2)}) collective-permute-start(bf16[128]{0:T(256)(128)(2,1)S(1)} %convert_bitcast_fusion), channel_id=1, source_target_pairs={{0,48},{16,64},{32,80},{48,96},{64,112},{80,128},{96,144},{112,160... | collective-permute-start | bytes 776 | tf_op jit(solution)/shard_map/ppermute | solution.py:21
  683.6 25.0 %collective-permute-start.4 = (bf16[128]{0:T(256)(128)(2,1)S(1)}, bf16[128]{0:T(256)(128)(2,1)}, u32[]{:S(2)}, u32[]{:S(2)}) collective-permute-start(bf16[128]{0:T(256)(128)(2,1)S(1)} %convert_bitcast_fusion), channel_id=1, source_target_pairs={{0,32},{16,48},{32,64},{48,80},{64,96},{80,112},{96,128},{112,144}... | collective-permute-start | bytes 776 | tf_op jit(solution)/shard_map/ppermute | solution.py:21
  687.3 21.4 %collective-permute-start.5 = (bf16[128]{0:T(256)(128)(2,1)S(1)}, bf16[128]{0:T(256)(128)(2,1)}, u32[]{:S(2)}, u32[]{:S(2)}) collective-permute-start(bf16[128]{0:T(256)(128)(2,1)S(1)} %convert_bitcast_fusion), channel_id=1, source_target_pairs={{0,16},{16,32},{32,48},{48,64},{64,80},{80,96},{96,112},{112,128},... | collective-permute-start | bytes 776 | tf_op jit(solution)/shard_map/ppermute | solution.py:21
  692.6 17.7 %collective-permute-start.6 = (bf16[128,512]{0,1:T(8,128)(2,1)}, bf16[128,512]{0,1:T(8,128)(2,1)S(1)}, u32[]{:S(2)}, u32[]{:S(2)}) collective-permute-start(bf16[128,512]{0,1:T(8,128)(2,1)} %bitcast.9), channel_id=1, source_target_pairs={{0,48},{16,64},{32,80},{48,96},{64,112},{80,128},{96,144},{112,160... | collective-permute-start | bytes 393224 | tf_op jit(solution)/shard_map/ppermute | solution.py:21
  696.7 15.2 %collective-permute-start.7 = (bf16[128,512]{0,1:T(8,128)(2,1)}, bf16[128,512]{0,1:T(8,128)(2,1)S(1)}, u32[]{:S(2)}, u32[]{:S(2)}) collective-permute-start(bf16[128,512]{0,1:T(8,128)(2,1)} %bitcast.9), channel_id=1, source_target_pairs={{0,32},{16,48},{32,64},{48,80},{64,96},{80,112},{96,128},{112,144}... | collective-permute-start | bytes 393224 | tf_op jit(solution)/shard_map/ppermute | solution.py:21
  704.0 9.6 %collective-permute-start.8 = (bf16[128,512]{0,1:T(8,128)(2,1)}, bf16[128,512]{0,1:T(8,128)(2,1)}, u32[]{:S(2)}, u32[]{:S(2)}) collective-permute-start(bf16[128,512]{0,1:T(8,128)(2,1)} %bitcast.9), channel_id=1, source_target_pairs={{0,16},{16,32},{32,48},{48,64},{64,80},{80,96},{96,112},{112,128},... | collective-permute-start | bytes 393224 | tf_op jit(solution)/shard_map/ppermute | solution.py:21
  710.2 0.6 copy-start.3
  711.9 0.6 copy-start.2
  720.7 154.2 %copy-start.4 = (pred[128,512]{0,1:T(8,128)(4,1)S(1)}, pred[128,512]{0,1:T(8,128)(4,1)}, u32[]{:S(2)}) copy-start(pred[128,512]{0,1:T(8,128)(4,1)} %and_and_fusion) | copy-start | bytes 196612
  860.3 14.6 %copy-start.1 = (f32[4,512,128,8]{2,1,3,0:T(8,128)S(1)}, f32[4,512,128,8]{2,1,3,0:T(8,128)}, u32[]{:S(2)}) copy-start(f32[4,512,128,8]{2,1,3,0:T(8,128)} %fusion.17) | copy-start | bytes 25165828
  865.1 15.6 %collective-permute-start = (bf16[128,512]{1,0:T(8,128)(2,1)S(1)}, bf16[128,512]{1,0:T(8,128)(2,1)S(1)}, u32[]{:S(2)}, u32[]{:S(2)}) collective-permute-start(bf16[128,512]{1,0:T(8,128)(2,1)S(1)} %fusion.14), channel_id=1, source_target_pairs={{0,48},{16,64},{32,80},{48,96},{64,112},{80,128},{96,144},{112,160... | collective-permute-start | bytes 393224 | tf_op jit(solution)/shard_map/ppermute | solution.py:21
  867.4 13.3 %collective-permute-start.1 = (bf16[128,512]{1,0:T(8,128)(2,1)S(1)}, bf16[128,512]{1,0:T(8,128)(2,1)S(1)}, u32[]{:S(2)}, u32[]{:S(2)}) collective-permute-start(bf16[128,512]{1,0:T(8,128)(2,1)S(1)} %fusion.14), channel_id=1, source_target_pairs={{0,32},{16,48},{32,64},{48,80},{64,96},{80,112},{96,128},{112,144}... | collective-permute-start | bytes 393224 | tf_op jit(solution)/shard_map/ppermute | solution.py:21
  869.8 10.9 %collective-permute-start.2 = (bf16[128,512]{1,0:T(8,128)(2,1)S(1)}, bf16[128,512]{1,0:T(8,128)(2,1)S(1)}, u32[]{:S(2)}, u32[]{:S(2)}) collective-permute-start(bf16[128,512]{1,0:T(8,128)(2,1)S(1)} %fusion.14), channel_id=1, source_target_pairs={{0,16},{16,32},{32,48},{48,64},{64,80},{80,96},{96,112},{112,128},... | collective-permute-start | bytes 393224 | tf_op jit(solution)/shard_map/ppermute | solution.py:21
  881.0 5.4 copy-start.5
Sparse Core Ops, SparseCore 0:
  12.4 631.7 reduce-scatter.1
  678.1 182.1 all-gather.1
where the time goes:
time: 904 us; the launch traced here: 894 us
  waiting for transfers between devices  777 us (86%)
  starting transfers between devices  34.3 us (4%)
  blocking collectives  32.3 us (4%)
  between operations  14.9 us (2%)
  matrix products  14.1 us (2%)
  other arithmetic  11.5 us (1%)
  local copies, waits for them, and re-layouts  10.9 us (1%)
    reduce_scatter x1, waiting for transfers between devices, on_device(): lax.psum_scatter(grad_terms.astype(jnp.bfloat16), 'dp', scatter_dimension...  636 us
    all_gather x1, waiting for transfers between devices, on_device(): lax.all_gather(group_rows, 'dp', axis=0, tiled=True)  140 us
    ppermute x9, starting transfers between devices, passed_along(): return lax.ppermute(block, axis, route)  34.2 us
    all_gather x1, blocking collectives, on_device(): group_rows = lax.all_gather(rounded_rows, 'replica', axis=0, tiled=True)  32.3 us
  transfers between devices with their start and end apart: 11, of which 2 were waited for; matrix products, arithmetic and copies ran while one was open for 2% of the time, Pallas kernels for 0%

commit v1 on v0

v1 whole, which is shorter than its diff:
```python
import functools

import jax
import jax.numpy as jnp
from jax import lax
from jax.experimental import pallas as pl
from jax.experimental.pallas import tpu as pltpu
from jax.sharding import PartitionSpec as P

HD = 128
NZ = 16
MESH = pl.DeviceIdType.MESH

beta_one = 0.9
beta_two = 0.95
bias_one = 1.0 - 0.9**10
bias_two = 1.0 - 0.95**10
adam_eps = 1e-08
learn_rate = 0.002
weight_decay = 0.1
LOG2E = 1.4426950408889634


def device_at(x, y, z, c):
    return (
        z * 2 + lax.div(x, jnp.int32(2)),
        y * 4 + lax.rem(x, jnp.int32(2)) * 2 + c,
    )


def wait_bytes(ref, sem):
    pltpu.make_async_copy(ref, ref, sem).wait()


def kernel(
    grad,
    master,
    moment_first,
    moment_second,
    queries,
    keys,
    hidden,
    segs,
    packed_len,
    master_out,
    first_out,
    second_out,
    attended,
    own_terms,
    pair_terms,
    pair_sums,
    z_terms,
    rounded,
    wbuf,
    hbuf,
    kbuf,
    segsrc,
    segbuf,
    bias,
    wts,
    tots,
    vout,
    vbuf,
    local_sem,
    send_sem,
    pair_sem,
    z_sem,
    hid_sem,
    key_sem,
    seg_sem,
    wz_sem,
    ring_sem,
    val_sem,
):
    i32 = jnp.int32
    dp = lax.axis_index("dp").astype(i32)
    rep = lax.axis_index("replica").astype(i32)
    z = lax.div(dp, i32(2))
    xh = lax.rem(dp, i32(2))
    y = lax.div(rep, i32(4))
    xl = lax.rem(lax.div(rep, i32(2)), i32(2))
    c = lax.rem(rep, i32(2))
    x = xh * 2 + xl

    def mod(value, n):
        return lax.rem(value + n, i32(n))

    def send(src, dst, s_sem, r_sem, device):
        copy = pltpu.make_async_remote_copy(
            src_ref=src,
            dst_ref=dst,
            send_sem=s_sem,
            recv_sem=r_sem,
            device_id=device,
            device_id_type=MESH,
        )
        copy.start()
        return copy

    hid_local = pltpu.make_async_copy(hidden, hbuf.at[c], local_sem.at[0])
    own_local = pltpu.make_async_copy(grad.at[:, xh], own_terms, local_sem.at[1])
    own_local.start()

    barrier = pltpu.get_barrier_semaphore()

    def greet(device):
        pl.semaphore_signal(barrier, inc=1, device_id=device, device_id_type=MESH)

    greet(device_at(mod(x + 2, 4), y, z, c))
    for step in (1, 3):
        greet(device_at(mod(x + step, 4), y, z, c))
        greet(device_at(x, mod(y + step, 4), z, c))

    def greet_z(d, carry):
        greet(device_at(x, y, mod(z + d, NZ), c))
        greet(device_at(x, y, mod(z + d, NZ), 1 - c))
        return carry

    lax.fori_loop(1, NZ, greet_z, 0)
    greet(device_at(x, y, z, 1 - c))
    other_x = mod(x + 2, 4)
    for shift in (1, 3, -1, -3):
        there = lax.div(mod(dp + shift, 32), i32(2))
        greet(device_at(other_x, y, there, 1 - c))
    for offset in (1, -1, 4 * xh - 2):
        greet(device_at(other_x, y, mod(z + offset, NZ), c))
    pl.semaphore_wait(barrier, 1 + 4 + 30 + 1 + 4 + 3)

    group_here = lax.div(z, i32(4))
    partner = device_at(other_x, y, z, c)
    order = (2, 1, 3, 0)
    for n, k in enumerate(order):
        g = mod(group_here + k, 4)
        rows = pl.ds(g * 4, 4)
        send(
            grad.at[rows, 1 - xh],
            pair_terms.at[rows],
            send_sem.at[0],
            pair_sem.at[n],
            partner,
        )

    sibling = device_at(x, y, z, 1 - c)
    hid_local.start()
    segsrc[...] = jnp.broadcast_to(segs[...], (8, 128))
    key_copies = []
    for o in (1, 2, 3):
        to = (mod(dp + o, 32), rep)
        key_copies.append(
            send(segsrc, segbuf.at[3 - o], seg_sem.at[3 + o - 1], seg_sem.at[o - 1], to)
        )
        key_copies.append(
            send(keys, kbuf.at[3 - o], key_sem.at[3 + o - 1], key_sem.at[o - 1], to)
        )
    hid_copy = send(hidden, hbuf.at[c], hid_sem.at[0], hid_sem.at[1], sibling)
    kbuf[3] = keys[...]
    segbuf[3] = segsrc[...]

    own_local.wait()
    for n, k in enumerate(order):
        g = mod(group_here + k, 4)
        rows = pl.ds(g * 4, 4)
        wait_bytes(pair_terms.at[rows], pair_sem.at[n])
        pair_sums[rows] = (
            own_terms[rows].astype(jnp.float32) + pair_terms[rows].astype(jnp.float32)
        ).astype(jnp.bfloat16)
        for i in range(1 if k == 0 else 0, 4):
            there = g * 4 + (mod(z + i, 4) if k == 0 else i)
            send(
                pair_sums.at[there],
                z_terms.at[z],
                send_sem.at[1],
                z_sem.at[0],
                device_at(x, y, there, c),
            )
    z_terms[z] = pair_sums[z]

    for copy in key_copies:
        copy.wait()
    seg_q = jnp.transpose(jnp.broadcast_to(segs[...], (128, 128)))
    row_id = lax.broadcasted_iota(i32, (128, 128), 0)
    col_id = lax.broadcasted_iota(i32, (128, 128), 1)
    for slot in range(4):
        o = 3 - slot
        same = seg_q == jnp.broadcast_to(segbuf[slot][0:1, :], (128, 128))
        if o == 0:
            allowed = same & (col_id <= row_id)
        else:
            allowed = same & (jnp.broadcast_to(dp, (128, 128)) >= o)
        bias[:, slot * 128 : (slot + 1) * 128] = jnp.where(allowed, 0.0, -1e30)

    def scores_of(head, carry):
        kv = lax.div(head, i32(8))
        q = queries[:, pl.ds(pl.multiple_of(head * HD, HD), HD)]
        k = kbuf[:, :, pl.ds(pl.multiple_of(kv * HD, HD), HD)].reshape(512, HD)
        s = lax.dot_general(
            q, k, (((1,), (1,)), ((), ())), preferred_element_type=jnp.float32
        )
        s = s + bias[...]
        top = jnp.max(s, axis=1, keepdims=True)
        w = jnp.exp2((s - top) * (HD**-0.5 * LOG2E))
        tots[head] = jnp.broadcast_to(jnp.sum(w, axis=1, keepdims=True), (128, HD))
        wts[head] = w.astype(jnp.bfloat16)
        return carry

    lax.fori_loop(0, 32, scores_of, 0)

    wait_bytes(z_terms.at[pl.ds(0, 15)], z_sem.at[0])
    grad_sum = jnp.sum(z_terms[...].astype(jnp.float32), axis=0)
    first_new = beta_one * moment_first[...] + (1.0 - beta_one) * grad_sum
    second_new = (
        beta_two * moment_second[...] + (1.0 - beta_two) * grad_sum * grad_sum
    )
    step_dir = (
        first_new / bias_one / (jnp.sqrt(second_new / bias_two) + adam_eps)
        + weight_decay * master[...]
    )
    master_new = master[...] - learn_rate * step_dir
    rows_new = master_new.astype(jnp.bfloat16)
    rounded[0] = rows_new[:, :256]
    rounded[1] = rows_new[:, 256:]

    own_rows = pl.ds(pl.multiple_of(c * 16, 16), 16)
    send(
        rounded.at[1 - c],
        wbuf.at[z, xh, y, xl, own_rows],
        send_sem.at[3],
        wz_sem.at[z],
        sibling,
    )
    for n, k in enumerate((0, 1, 3, 2)):
        g = mod(group_here + k, 4)
        for i in range(1 if k == 0 else 0, 4):
            there = g * 4 + (mod(z + i, 4) if k == 0 else i)
            send(
                rounded.at[c],
                wbuf.at[z, xh, y, xl, own_rows],
                send_sem.at[2],
                wz_sem.at[z],
                device_at(x, y, there, c),
            )
            send(
                rounded.at[1 - c],
                wbuf.at[z, xh, y, xl, own_rows],
                send_sem.at[3],
                wz_sem.at[z],
                device_at(x, y, there, 1 - c),
            )
    wbuf[z, xh, y, xl, own_rows] = rounded[c]
    master_out[...] = master_new
    first_out[...] = first_new
    second_out[...] = second_new

    near_x = (device_at(mod(x + 1, 4), y, z, c), device_at(mod(x + 3, 4), y, z, c))
    near_y = (device_at(x, mod(y + 1, 4), z, c), device_at(x, mod(y + 3, 4), z, c))

    def x_split(value):
        return lax.div(value, i32(2)), lax.rem(value, i32(2))

    gather_order = (0, 1, 3, 2)

    def group_of(n):
        return mod(group_here + gather_order[n], 4)

    def first_stage(n):
        g = group_of(n)
        if n == 0:
            wait_bytes(wbuf.at[z, xh, y, xl, pl.ds(0, 16)], wz_sem.at[z])
            for i in range(1, 4):
                zi = g * 4 + mod(z + i, 4)
                wait_bytes(wbuf.at[zi, xh, y, xl], wz_sem.at[zi])
        else:
            for i in range(4):
                zi = g * 4 + i
                wait_bytes(wbuf.at[zi, xh, y, xl], wz_sem.at[zi])
        for colour, near in ((0, near_x), (1, near_y)):
            part = wbuf.at[pl.ds(g * 4 + 2 * colour, 2), xh, y, xl]
            for way in (0, 1):
                send(part, part, send_sem.at[4], ring_sem.at[0, n, colour, way], near[way])

    def first_forward(n):
        g = group_of(n)
        for colour, near in ((0, near_x), (1, near_y)):
            for way in (0, 1):
                back = 3 if way == 0 else 1
                if colour == 0:
                    fh, fl = x_split(mod(x + back, 4))
                    fy = y
                else:
                    fh, fl, fy = xh, xl, mod(y + back, 4)
                zs = pl.ds(g * 4 + 2 * colour, 2)
                wait_bytes(wbuf.at[zs, fh, fy, fl], ring_sem.at[0, n, colour, way])
                part = wbuf.at[g * 4 + 2 * colour + way, fh, fy, fl]
                send(part, part, send_sem.at[5], ring_sem.at[1, n, colour, way], near[way])

    def second_stage(n):
        g = group_of(n)
        for colour, near in ((0, near_y), (1, near_x)):
            for way in (0, 1):
                if colour == 0:
                    fh, fl = x_split(mod(x + 2, 4))
                    fy = y
                else:
                    fh, fl, fy = xh, xl, mod(y + 2, 4)
                wait_bytes(
                    wbuf.at[g * 4 + 2 * colour + way, fh, fy, fl],
                    ring_sem.at[1, n, colour, way],
                )
            zs = pl.ds(g * 4 + 2 * colour, 2)
            part = wbuf.at[zs, :, y, :] if colour == 0 else wbuf.at[zs, xh, :, xl]
            for way in (0, 1):
                send(part, part, send_sem.at[6], ring_sem.at[2, n, colour, way], near[way])

    def second_forward(n):
        g = group_of(n)
        for colour, near in ((0, near_y), (1, near_x)):
            for way in (0, 1):
                back = 3 if way == 0 else 1
                zs = pl.ds(g * 4 + 2 * colour, 2)
                one = g * 4 + 2 * colour + way
                if colour == 0:
                    fy = mod(y + back, 4)
                    whole, part = wbuf.at[zs, :, fy, :], wbuf.at[one, :, fy, :]
                else:
                    fh, fl = x_split(mod(x + back, 4))
                    whole, part = wbuf.at[zs, fh, :, fl], wbuf.at[one, fh, :, fl]
                wait_bytes(whole, ring_sem.at[2, n, colour, way])
                send(part, part, send_sem.at[7], ring_sem.at[3, n, colour, way], near[way])

    def multiply(n, total):
        g = group_of(n)
        for colour in (0, 1):
            for way in (0, 1):
                one = g * 4 + 2 * colour + way
                if colour == 0:
                    part = wbuf.at[one, :, mod(y + 2, 4), :]
                else:
                    fh, fl = x_split(mod(x + 2, 4))
                    part = wbuf.at[one, fh, :, fl]
                wait_bytes(part, ring_sem.at[3, n, colour, way])

        def add(i, acc):
            zi = g * 4 + i
            cols = pl.ds(pl.multiple_of(zi * 512, 512), 512)
            return acc + jnp.dot(
                hbuf[:, :, cols].reshape(256, 512),
                wbuf[zi].reshape(512, 256),
                preferred_element_type=jnp.float32,
            )

        return lax.fori_loop(0, 4, add, total)

    total = jnp.zeros((256, 256), jnp.float32)
    for slot in range(8):
        if slot < 4:
            first_stage(slot)
        if 0 <= slot - 1 < 4:
            first_forward(slot - 1)
        if 0 <= slot - 2 < 4:
            second_stage(slot - 2)
        if 0 <= slot - 3 < 4:
            second_forward(slot - 3)
        if slot == 3:
            hid_local.wait()
            hid_copy.wait()
        if 0 <= slot - 4 < 4:
            total = multiply(slot - 4, total)

    vout[...] = total.astype(jnp.bfloat16).reshape(2, 128, 256)
    val_copies = []
    for o in (3, 2, 1, 0):
        there = mod(dp + o, 32)
        for other in (0, 1) if o else (1,):
            core = lax.rem(c + other, i32(2))
            val_copies.append(
                send(
                    vout.at[core],
                    vbuf.at[c, 3 - o],
                    val_sem.at[0, o, other],
                    val_sem.at[1, o, other],
                    (there, rep - c + core),
                )
            )
    vbuf[c, 3] = vout[c]

    wait_bytes(pair_terms, send_sem.at[0])
    wait_bytes(z_terms.at[pl.ds(0, 15)], send_sem.at[1])
    wait_bytes(wbuf.at[pl.ds(0, 15), 0, 0, 0, pl.ds(0, 16)], send_sem.at[2])
    wait_bytes(wbuf.at[pl.ds(0, 16), 0, 0, 0, pl.ds(0, 16)], send_sem.at[3])
    wait_bytes(wbuf.at[pl.ds(0, 2)], send_sem.at[4])
    wait_bytes(wbuf.at[pl.ds(0, 1)], send_sem.at[5])
    wait_bytes(wbuf.at[pl.ds(0, 8)], send_sem.at[6])
    wait_bytes(wbuf.at[pl.ds(0, 4)], send_sem.at[7])
    for copy in val_copies:
        copy.wait()

    pos = dp * 128 + lax.broadcasted_iota(i32, (128, HD), 0)
    live = pos < packed_len[0]
    for kv in range(4):
        v = vbuf[kv // 2, :, :, (kv % 2) * HD : (kv % 2 + 1) * HD].reshape(512, HD)

        def mix(j, carry):
            head = kv * 8 + j
            out = jnp.dot(wts[head], v, preferred_element_type=jnp.float32)
            out = jnp.where(live, out / tots[head], 0.0).astype(jnp.bfloat16)
            attended[:, pl.ds(pl.multiple_of(head * HD, HD), HD)] = out
            return carry

        lax.fori_loop(0, 8, mix, 0)


def on_device(
    grad_parts,
    master_weight,
    moment_one,
    moment_two,
    queries,
    keys_in,
    hidden,
    segment_ids,
    packed_len,
):
    bf16, f32 = jnp.bfloat16, jnp.float32
    any_spec = pl.BlockSpec(memory_space=pl.ANY)
    vmem = pl.BlockSpec(memory_space=pltpu.VMEM)
    smem = pl.BlockSpec(memory_space=pltpu.SMEM)
    dma = pltpu.SemaphoreType.DMA
    rows = jax.ShapeDtypeStruct((16, 512), f32)
    new_master, new_first, new_second, attended = pl.pallas_call(
        kernel,
        out_shape=(rows, rows, rows, jax.ShapeDtypeStruct((128, 4096), bf16)),
        in_specs=[any_spec, vmem, vmem, vmem, vmem, vmem, any_spec, vmem, smem],
        out_specs=(vmem, vmem, vmem, vmem),
        scratch_shapes=[
            pltpu.VMEM((NZ, 16, 512), bf16),
            pltpu.VMEM((NZ, 16, 512), bf16),
            pltpu.VMEM((NZ, 16, 512), bf16),
            pltpu.VMEM((NZ, 16, 512), bf16),
            pltpu.VMEM((2, 16, 256), bf16),
            pltpu.VMEM((NZ, 2, 4, 2, 32, 256), bf16),
            pltpu.VMEM((2, 128, 8192), bf16),
            pltpu.VMEM((4, 128, 512), bf16),
            pltpu.VMEM((8, 128), jnp.int32),
            pltpu.VMEM((4, 8, 128), jnp.int32),
            pltpu.VMEM((128, 512), f32),
            pltpu.VMEM((32, 128, 512), bf16),
            pltpu.VMEM((32, 128, HD), f32),
            pltpu.VMEM((2, 128, 256), bf16),
            pltpu.VMEM((2, 4, 128, 256), bf16),
            dma((2,)),
            dma((8,)),
            dma((4,)),
            dma((1,)),
            dma((2,)),
            dma((6,)),
            dma((6,)),
            dma((NZ,)),
            dma((4, 4, 2, 2)),
            dma((2, 4, 2)),
        ],
        compiler_params=pltpu.CompilerParams(
            collective_id=0, has_side_effects=True, vmem_limit_bytes=48 << 20
        ),
    )(
        grad_parts.reshape(NZ, 2, 16, 512),
        master_weight,
        moment_one,
        moment_two,
        queries[0],
        keys_in[0],
        hidden[0],
        segment_ids,
        packed_len,
    )
    return (new_master, new_first, new_second, attended[None])


def solution(mesh):
    in_specs = (
        P("dp", "replica", None),
        P(("dp", "replica"), None),
        P(("dp", "replica"), None),
        P(("dp", "replica"), None),
        P("replica", "dp", None),
        P("replica", "dp", None),
        P("replica", "dp", None),
        P("replica", "dp"),
        P("replica"),
    )
    out_specs = (
        P(("dp", "replica"), None),
        P(("dp", "replica"), None),
        P(("dp", "replica"), None),
        P("replica", "dp", None),
    )
    return jax.shard_map(
        on_device, mesh=mesh, in_specs=in_specs, out_specs=out_specs, check_vma=False
    )
```

time: 904 us -> 118 us (0.13)
  waiting for transfers between devices: 777 us -> 0 us
  Pallas kernels: 0 us -> 105 us
  starting transfers between devices: 34.3 us -> 0 us
  blocking collectives: 32.3 us -> 0 us
  matrix products: 14.1 us -> 0 us
  between operations: 14.9 us -> 1.31 us
  other arithmetic: 11.5 us -> 0 us
    reduce_scatter x1 -> x0, waiting for transfers between devices: 636 us -> none  [on_device(): lax.psum_scatter(grad_terms.astype(jnp.bfloat16), 'dp', scatter_dimension...]
    all_gather x1 -> x0, waiting for transfers between devices: 140 us -> none  [on_device(): lax.all_gather(group_rows, 'dp', axis=0, tiled=True)]
    pallas_call x0 -> x1, Pallas kernels: none -> 105 us  [on_device(): pl.pallas_call(kernel, out_shape=(rows, rows, rows, jax.ShapeDtypeStruct(...]
    ppermute x9 -> x0, starting transfers between devices: 34.2 us -> none  [passed_along(): return lax.ppermute(block, axis, route)]
    all_gather x1 -> x0, blocking collectives: 32.3 us -> none  [on_device(): group_rows = lax.all_gather(rounded_rows, 'replica', axis=0, tiled=True)]
    dot_general x3 -> x0, matrix products: 14.1 us -> none  [the longest x1 5.41 us: prefill(): jnp.einsum('qhgd,khd->hgqk', query_heads, all_keys, preferred_element_typ...]
  transfers between devices with their start and end apart: 11 -> 0, of which waited for: 2 -> 0; matrix products, arithmetic and copies ran while one was open for 2% -> 0% of each run, Pallas kernels for 0% -> 0%
where the time goes in v1:
time: 118 us; the launch traced here: 117 us
  Pallas kernels  105 us (89%)
  local copies, waits for them, and re-layouts  10.5 us (9%)
  between operations  1.31 us (1%)
    pallas_call x1, Pallas kernels, on_device(): pl.pallas_call(kernel, out_shape=(rows, rows, rows, jax.ShapeDtypeStruct(...  105 us
    unnamed x20, local copies, waits for them, and re-layouts  10.5 us

profile of v1, /device:TPU:1, one launch (start us, length us, event | category | flops | bytes accessed | tf_op | source)
XLA Modules:
  0.0 117.2 jit_solution(2557970861725862881)
XLA Ops:
  1.3 0.0 copy-start
  1.3 1.6 %copy-done = bf16[1,128,8192]{2,1,0:T(8,128)(2,1)S(1)} copy-done((bf16[1,128,8192]{2,1,0:T(8,128)(2,1)S(1)}, bf16[1,128,8192]{2,1,0:T(8,128)(2,1)}, u32[]{:S(2)}) %copy-start) | copy-done | bytes 2097176
  2.9 0.0 copy-start.1
  2.9 1.2 %copy-done.1 = bf16[1,128,4096]{2,1,0:T(8,128)(2,1)S(1)} copy-done((bf16[1,128,4096]{2,1,0:T(8,128)(2,1)S(1)}, bf16[1,128,4096]{2,1,0:T(8,128)(2,1)}, u32[]{:S(2)}) %copy-start.1) | copy-done | bytes 1048600
  4.1 0.0 copy-start.2
  4.1 1.0 copy-done.2
  5.1 0.0 copy-start.3
  5.1 0.9 copy-done.3
  6.0 0.0 copy-start.4
  6.0 0.8 copy-done.4
  6.8 0.0 copy-start.5
  6.8 0.8 copy-done.5
  7.6 0.0 copy-start.6
  7.6 0.8 copy-done.6
  8.3 0.0 copy-start.7
  8.3 0.7 copy-done.7
  9.0 105.4 %shard_map.120 = (f32[16,512]{1,0:T(8,128)S(1)}, f32[16,512]{1,0:T(8,128)S(1)}, f32[16,512]{1,0:T(8,128)S(1)}, bf16[128,4096]{1,0:T(8,128)(2,1)S(1)}) custom-call(bf16[16,2,16,512]{3,2,1,0:T(8,128)(2,1)S(1)} %bitcast.8, f32[16,512]{1,0:T(8,128)S(1)} %copy-done.4, f32[16,512]{1,0:T(8,128)S(1)} %copy-done.5, f32[16,512]{1,0:T(8,128)S(1)} %copy-done.6, ...), custom_call_target="tpu_custom_call" | custom-call | tf_op jit(solution)/shard_map/pallas_call | solution.py:429
  114.3 0.6 copy.18
  115.0 0.6 copy.19
  115.6 0.6 copy.20
  116.2 1.0 copy.21
Async XLA Ops:
  1.3 1.6 %copy-start = (bf16[1,128,8192]{2,1,0:T(8,128)(2,1)S(1)}, bf16[1,128,8192]{2,1,0:T(8,128)(2,1)}, u32[]{:S(2)}) copy-start(bf16[1,128,8192]{2,1,0:T(8,128)(2,1)} %param.15) | copy-start | bytes 6291460
  2.9 1.2 %copy-start.1 = (bf16[1,128,4096]{2,1,0:T(8,128)(2,1)S(1)}, bf16[1,128,4096]{2,1,0:T(8,128)(2,1)}, u32[]{:S(2)}) copy-start(bf16[1,128,4096]{2,1,0:T(8,128)(2,1)} %param.13) | copy-start | bytes 3145732
  4.1 1.0 copy-start.2
  5.1 0.9 copy-start.3
  6.0 0.8 copy-start.4
  6.8 0.8 copy-start.5
  7.6 0.8 copy-start.6
  8.3 0.7 copy-start.7

commit v2 on v0

v2 whole, which is shorter than its diff:
```python
import jax
import jax.numpy as jnp
from jax import lax
from jax.experimental import pallas as pl
from jax.experimental.pallas import tpu as pltpu
from jax.sharding import PartitionSpec as P

HD = 128
NZ = 16
MESH = pl.DeviceIdType.MESH

beta_one = 0.9
beta_two = 0.95
bias_one = 1.0 - 0.9**10
bias_two = 1.0 - 0.95**10
adam_eps = 1e-08
learn_rate = 0.002
weight_decay = 0.1
LOG2E = 1.4426950408889634
UNROLL_S = 4
UNROLL_M = 8
UNROLL_W = 2
LAST = 3


def adam_update(grad_sum, master, moment_first, moment_second):
    first_new = beta_one * moment_first + (1.0 - beta_one) * grad_sum
    second_new = beta_two * moment_second + (1.0 - beta_two) * grad_sum * grad_sum
    step_dir = (
        first_new / bias_one / (jnp.sqrt(second_new / bias_two) + adam_eps)
        + weight_decay * master
    )
    master_new = master - learn_rate * step_dir
    return master_new, first_new, second_new, master_new.astype(jnp.bfloat16)


def device_at(x, y, z, c):
    return (
        z * 2 + lax.div(x, jnp.int32(2)),
        y * 4 + lax.rem(x, jnp.int32(2)) * 2 + c,
    )


def wait_bytes(ref, sem):
    pltpu.make_async_copy(ref, ref, sem).wait()


def kernel(
    grad,
    master_in,
    first_in,
    second_in,
    queries_in,
    keys_in,
    hidden,
    segs_in,
    packed_in,
    grad_out,
    attended,
    master,
    moment_first,
    moment_second,
    queries,
    segs,
    packed_len,
    own_terms,
    pair_terms,
    pair_sums,
    z_terms,
    rounded,
    wbuf,
    hbuf,
    kbuf,
    kpair,
    segsrc,
    segbuf,
    bias,
    wts,
    tots,
    vout,
    vbuf,
    local_sem,
    send_sem,
    pair_sem,
    z_sem,
    hid_sem,
    key_sem,
    seg_sem,
    wz_sem,
    ring_sem,
    val_sem,
):
    i32 = jnp.int32
    dp = lax.axis_index("dp").astype(i32)
    rep = lax.axis_index("replica").astype(i32)
    z = lax.div(dp, i32(2))
    xh = lax.rem(dp, i32(2))
    y = lax.div(rep, i32(4))
    xl = lax.rem(lax.div(rep, i32(2)), i32(2))
    c = lax.rem(rep, i32(2))
    x = xh * 2 + xl

    def mod(value, n):
        return lax.rem(value + n, i32(n))

    def send(src, dst, s_sem, r_sem, device):
        copy = pltpu.make_async_remote_copy(
            src_ref=src,
            dst_ref=dst,
            send_sem=s_sem,
            recv_sem=r_sem,
            device_id=device,
            device_id_type=MESH,
        )
        copy.start()
        return copy

    barrier = pltpu.get_barrier_semaphore()

    def greet(device):
        pl.semaphore_signal(barrier, inc=1, device_id=device, device_id_type=MESH)

    def greet_z(d, carry):
        greet(device_at(x, y, mod(z + d, NZ), c))
        greet(device_at(x, y, mod(z + d, NZ), 1 - c))
        return carry

    lax.fori_loop(1, NZ, greet_z, 0)
    sibling = device_at(x, y, z, 1 - c)
    other_x = mod(x + 2, 4)
    greet(sibling)
    for step in (1, 2, 3):
        greet(device_at(mod(x + step, 4), y, z, c))
        greet(device_at(x, mod(y + step, 4), z, c))
    for offset in (1, -1, 4 * xh - 2):
        greet(device_at(other_x, y, mod(z + offset, NZ), c))
    for offset in (0, 1, -1, 4 * xh - 2):
        greet(device_at(other_x, y, mod(z + offset, NZ), 1 - c))

    def local(n, src, dst):
        copy = pltpu.make_async_copy(src, dst, local_sem.at[n])
        copy.start()
        return copy

    own_local = local(0, grad.at[:, xh], own_terms)
    seg_local = local(1, segs_in, segs)
    state_local = (
        local(2, master_in, master),
        local(3, first_in, moment_first),
        local(4, second_in, moment_second),
    )
    late_local = (
        local(5, packed_in, packed_len),
        local(6, queries_in, queries),
        local(7, keys_in, kbuf.at[3]),
        local(8, hidden, hbuf.at[c]),
    )
    pl.semaphore_wait(barrier, 30 + 1 + 6 + 3 + 4)

    half_here = lax.div(z, i32(8))
    partner = device_at(other_x, y, z, c)

    def half_of(n):
        return lax.rem(half_here + n, i32(2))

    for p in (0, 1):
        for n in (1, 0):
            rows = pl.ds(half_of(n) * 8, 8)
            send(
                grad.at[rows, 1 - xh, :, pl.ds(p * 256, 256)],
                pair_terms.at[p, rows],
                send_sem.at[0],
                pair_sem.at[p, n],
                partner,
            )

    hid_copy = send(hidden, hbuf.at[c], hid_sem.at[0], hid_sem.at[1], sibling)
    pair_keys = send(keys_in, kpair, key_sem.at[4], key_sem.at[0], partner)
    seg_local.wait()
    segsrc[...] = jnp.broadcast_to(segs[...], (8, 128))
    segbuf[3] = segsrc[...]
    seg_copies = []
    for o in (1, 2, 3):
        seg_copies.append(
            send(
                segsrc,
                segbuf.at[3 - o],
                seg_sem.at[3 + o - 1],
                seg_sem.at[o - 1],
                (mod(dp + o, 32), rep),
            )
        )

    def z_partners(n):
        g = half_of(n)
        for i in range(1 if n == 0 else 0, 8):
            yield g * 8 + (lax.rem(z + i, i32(8)) if n == 0 else i)

    own_local.wait()
    for p in (0, 1):
        for n in (1, 0):
            rows = pl.ds(half_of(n) * 8, 8)
            wait_bytes(pair_terms.at[p, rows], pair_sem.at[p, n])
            own = own_terms[rows, :, p * 256 : (p + 1) * 256].astype(jnp.float32)
            pair_sums[p, rows] = (own + pair_terms[p, rows].astype(jnp.float32)).astype(
                jnp.bfloat16
            )
            for there in z_partners(n):
                send(
                    pair_sums.at[p, there],
                    z_terms.at[p, z],
                    send_sem.at[1],
                    z_sem.at[p],
                    device_at(x, y, there, c),
                )
        z_terms[p, z] = pair_sums[p, z]
    for copy in state_local:
        copy.wait()

    own_rows = pl.ds(pl.multiple_of(c * 16, 16), 16)

    def update(p):
        cols = slice(p * 256, (p + 1) * 256)
        wait_bytes(z_terms.at[p, pl.ds(0, 15)], z_sem.at[p])
        grad_sum = jnp.sum(z_terms[p].astype(jnp.float32), axis=0)
        rows_new = adam_update(
            grad_sum, master[:, cols], moment_first[:, cols], moment_second[:, cols]
        )[3]
        rounded[p, 0] = rows_new[:, :128]
        rounded[p, 1] = rows_new[:, 128:]
        mine = wbuf.at[p, z, xh, y, xl, own_rows]
        arrived = wz_sem.at[p, z]
        send(rounded.at[p, 1 - c], mine, send_sem.at[3], arrived, sibling)
        for n in (0, 1):
            for there in z_partners(n):
                to, across = device_at(x, y, there, c), device_at(x, y, there, 1 - c)
                send(rounded.at[p, c], mine, send_sem.at[2], arrived, to)
                send(rounded.at[p, 1 - c], mine, send_sem.at[3], arrived, across)
        wbuf[p, z, xh, y, xl, own_rows] = rounded[p, c]
        grad_out[:, cols] = grad_sum

    steps = (1, 3, 2)
    near_x = [device_at(mod(x + step, 4), y, z, c) for step in steps]
    near_y = [device_at(x, mod(y + step, 4), z, c) for step in steps]

    def x_split(value):
        return lax.div(value, i32(2)), lax.rem(value, i32(2))

    def four(n, colour):
        return pl.ds(half_of(n) * 8 + 4 * colour, 4)

    def two(n, colour, way):
        return pl.ds(half_of(n) * 8 + 4 * colour + 2 * way, 2)

    def column_at(colour, back):
        if colour == 0:
            fh, fl = x_split(mod(x + back, 4))
            return fh, y, fl
        return xh, mod(y + back, 4), xl

    def line_at(p, zs, colour, back):
        if colour == 0:
            return wbuf.at[p, zs, :, mod(y + back, 4), :]
        fh, fl = x_split(mod(x + back, 4))
        return wbuf.at[p, zs, fh, :, fl]

    def first_stage(r):
        p, n = r // 2, r % 2
        if n == 0:
            wait_bytes(wbuf.at[p, z, xh, y, xl, pl.ds(0, 16)], wz_sem.at[p, z])
        for zi in z_partners(n):
            wait_bytes(wbuf.at[p, zi, xh, y, xl], wz_sem.at[p, zi])
        for colour, near in ((0, near_x), (1, near_y)):
            part = wbuf.at[p, four(n, colour), xh, y, xl]
            for way in (2, 0, 1):
                send(part, part, send_sem.at[4], ring_sem.at[0, r, colour, way], near[way])

    def second_stage(r):
        p, n = r // 2, r % 2
        ways = (2, 0, 1) if r == LAST else (0, 1)
        for colour, near in ((0, near_y), (1, near_x)):
            for way in (0, 1, 2):
                fh, fy, fl = column_at(colour, 4 - steps[way])
                wait_bytes(
                    wbuf.at[p, four(n, colour), fh, fy, fl], ring_sem.at[0, r, colour, way]
                )
            part = line_at(p, four(n, colour), colour, 0)
            for way in ways:
                send(part, part, send_sem.at[5], ring_sem.at[1, r, colour, way], near[way])

    def second_forward(r):
        p, n = r // 2, r % 2
        for colour, near in ((0, near_y), (1, near_x)):
            for way in (0, 1):
                back = 4 - steps[way]
                wait_bytes(
                    line_at(p, four(n, colour), colour, back), ring_sem.at[1, r, colour, way]
                )
                part = line_at(p, two(n, colour, way), colour, back)
                send(part, part, send_sem.at[6], ring_sem.at[2, r, colour, way], near[way])

    def multiply(r, total):
        p, n = r // 2, r % 2
        for colour in (0, 1):
            if r == LAST:
                for way in (0, 1, 2):
                    wait_bytes(
                        line_at(p, four(n, colour), colour, 4 - steps[way]),
                        ring_sem.at[1, r, colour, way],
                    )
            else:
                for way in (0, 1):
                    wait_bytes(
                        line_at(p, two(n, colour, way), colour, 2),
                        ring_sem.at[2, r, colour, way],
                    )
        g = half_of(n)

        def add(i, acc):
            zi = g * 8 + i
            cols = pl.ds(pl.multiple_of(zi * 512, 512), 512)
            return acc + jnp.dot(
                hbuf[:, :, cols].reshape(256, 512),
                wbuf[p, zi].reshape(512, 128),
                preferred_element_type=jnp.float32,
            )

        return lax.fori_loop(0, 8, add, total, unroll=UNROLL_W)

    val_copies = ([], [])

    def send_values(p, total):
        vout[p] = total.astype(jnp.bfloat16).reshape(2, 128, 128)
        for o in (3, 2, 1, 0):
            for other in (0, 1) if o else (1,):
                core = lax.rem(c + other, i32(2))
                val_copies[p].append(
                    send(
                        vout.at[p, core],
                        vbuf.at[p, 3 - o, c],
                        val_sem.at[p, 0, o, other],
                        val_sem.at[p, 1, o, other],
                        (mod(dp + o, 32), rep - c + core),
                    )
                )
        vbuf[p, 3, c] = vout[p, c]

    def scores_of(head, carry):
        kv = lax.div(head, i32(8))
        q = queries[:, pl.ds(pl.multiple_of(head * HD, HD), HD)]
        k = kbuf[:, :, pl.ds(pl.multiple_of(kv * HD, HD), HD)].reshape(512, HD)
        s = lax.dot_general(
            q, k, (((1,), (1,)), ((), ())), preferred_element_type=jnp.float32
        )
        s = s + bias[...]
        top = jnp.max(s, axis=1, keepdims=True)
        w = jnp.exp2((s - top) * (HD**-0.5 * LOG2E))
        tots[head] = jnp.broadcast_to(jnp.sum(w, axis=1, keepdims=True), (128, HD))
        wts[head] = w.astype(jnp.bfloat16)
        return carry

    def scores(first, last):
        lax.fori_loop(first, last, scores_of, 0, unroll=UNROLL_S)

    def make_bias():
        for copy in seg_copies + key_copies:
            copy.wait()
        pair_keys.wait_send()

        @pl.when(xh == 0)
        def _():
            far_keys().wait()

        @pl.when(xh == 1)
        def _():
            kbuf[2] = kpair[...]

        seg_q = jnp.transpose(jnp.broadcast_to(segs[...], (128, 128)))
        row_id = lax.broadcasted_iota(i32, (128, 128), 0)
        col_id = lax.broadcasted_iota(i32, (128, 128), 1)
        for slot in range(4):
            o = 3 - slot
            same = seg_q == jnp.broadcast_to(segbuf[slot][0:1, :], (128, 128))
            if o == 0:
                allowed = same & (col_id <= row_id)
            else:
                allowed = same & (jnp.broadcast_to(dp, (128, 128)) >= o)
            bias[:, slot * 128 : (slot + 1) * 128] = jnp.where(allowed, 0.0, -1e30)

    def mix_heads(p):
        pos = dp * 128 + lax.broadcasted_iota(i32, (128, HD), 0)
        live = pos < packed_len[0]
        for core in (0, 1):
            v = vbuf[p, :, core].reshape(512, HD)

            def mix(j, carry):
                head = (2 * p + core) * 8 + j
                out = jnp.dot(wts[head], v, preferred_element_type=jnp.float32)
                out = jnp.where(live, out / tots[head], 0.0).astype(jnp.bfloat16)
                attended[:, pl.ds(pl.multiple_of(head * HD, HD), HD)] = out
                return carry

            lax.fori_loop(0, 8, mix, 0, unroll=UNROLL_M)

    key_copies = []

    def far_keys():
        return pltpu.make_async_remote_copy(
            src_ref=kpair,
            dst_ref=kbuf.at[0],
            send_sem=key_sem.at[7],
            recv_sem=key_sem.at[3],
            device_id=device_at(x, y, mod(z + 2, NZ), c),
            device_id_type=MESH,
        )

    def send_keys():
        pair_keys.wait_recv()
        next_z = device_at(x, y, mod(z + 1, NZ), c)

        @pl.when(xh == 0)
        def _():
            far_keys().start()

        key_copies.append(send(keys_in, kbuf.at[1], key_sem.at[5], key_sem.at[1], next_z))
        key_copies.append(
            send(kpair, kbuf.at[2 - 2 * xh], key_sem.at[6], key_sem.at[2], next_z)
        )

    zero = jnp.zeros((256, 128), jnp.float32)
    update(0)
    update(1)
    send_keys()
    first_stage(0)
    first_stage(1)
    second_stage(0)
    first_stage(2)
    second_stage(1)
    first_stage(3)
    for copy in late_local:
        copy.wait()
    hid_copy.wait()
    second_forward(0)
    second_stage(2)
    second_forward(1)
    total = multiply(0, zero)
    second_stage(3)
    total = multiply(1, total)
    send_values(0, total)
    second_forward(2)
    make_bias()
    scores(0, 8)
    total = multiply(2, zero)
    total = multiply(3, total)
    send_values(1, total)
    scores(8, 32)
    for copy in val_copies[0]:
        copy.wait()
    mix_heads(0)

    half = pl.ds(0, 16)
    wait_bytes(pair_terms, send_sem.at[0])
    wait_bytes(z_terms.at[:, pl.ds(0, 15)], send_sem.at[1])
    wait_bytes(wbuf.at[:, pl.ds(0, 15), 0, 0, 0, half], send_sem.at[2])
    wait_bytes(wbuf.at[:, :, 0, 0, 0, half], send_sem.at[3])
    wait_bytes(wbuf.at[0, pl.ds(0, 6)], send_sem.at[4])
    wait_bytes(wbuf.at[:, pl.ds(0, 9)], send_sem.at[5])
    wait_bytes(wbuf.at[0, pl.ds(0, 6)], send_sem.at[6])
    for copy in val_copies[1]:
        copy.wait()
    mix_heads(1)


def on_device(
    grad_parts,
    master_weight,
    moment_one,
    moment_two,
    queries,
    keys_in,
    hidden,
    segment_ids,
    packed_len,
):
    bf16, f32 = jnp.bfloat16, jnp.float32
    hbm = pl.BlockSpec(memory_space=pltpu.HBM)
    vmem = pl.BlockSpec(memory_space=pltpu.VMEM)
    dma = pltpu.SemaphoreType.DMA
    grad_sum, attended = pl.pallas_call(
        kernel,
        out_shape=(
            jax.ShapeDtypeStruct((16, 512), f32),
            jax.ShapeDtypeStruct((128, 4096), bf16),
        ),
        in_specs=[hbm] * 9,
        out_specs=(vmem, vmem),
        scratch_shapes=[
            pltpu.VMEM((16, 512), f32),
            pltpu.VMEM((16, 512), f32),
            pltpu.VMEM((16, 512), f32),
            pltpu.VMEM((128, 4096), bf16),
            pltpu.VMEM((1, 128), jnp.int32),
            pltpu.SMEM((1,), jnp.int32),
            pltpu.VMEM((NZ, 16, 512), bf16),
            pltpu.VMEM((2, NZ, 16, 256), bf16),
            pltpu.VMEM((2, NZ, 16, 256), bf16),
            pltpu.VMEM((2, NZ, 16, 256), bf16),
            pltpu.VMEM((2, 2, 16, 128), bf16),
            pltpu.VMEM((2, NZ, 2, 4, 2, 32, 128), bf16),
            pltpu.VMEM((2, 128, 8192), bf16),
            pltpu.VMEM((4, 128, 512), bf16),
            pltpu.VMEM((128, 512), bf16),
            pltpu.VMEM((8, 128), jnp.int32),
            pltpu.VMEM((4, 8, 128), jnp.int32),
            pltpu.VMEM((128, 512), f32),
            pltpu.VMEM((32, 128, 512), bf16),
            pltpu.VMEM((32, 128, HD), f32),
            pltpu.VMEM((2, 2, 128, 128), bf16),
            pltpu.VMEM((2, 4, 2, 128, 128), bf16),
            dma((9,)),
            dma((8,)),
            dma((2, 2)),
            dma((2,)),
            dma((2,)),
            dma((8,)),
            dma((6,)),
            dma((2, NZ)),
            dma((3, 4, 2, 3)),
            dma((2, 2, 4, 2)),
        ],
        compiler_params=pltpu.CompilerParams(
            collective_id=0, has_side_effects=True, vmem_limit_bytes=64 << 20
        ),
    )(
        grad_parts.reshape(NZ, 2, 16, 512),
        master_weight,
        moment_one,
        moment_two,
        queries[0],
        keys_in[0],
        hidden[0],
        segment_ids,
        packed_len,
    )
    new_master, new_first, new_second, _ = adam_update(
        grad_sum, master_weight, moment_one, moment_two
    )
    return (new_master, new_first, new_second, attended[None])


def solution(mesh):
    in_specs = (
        P("dp", "replica", None),
        P(("dp", "replica"), None),
        P(("dp", "replica"), None),
        P(("dp", "replica"), None),
        P("replica", "dp", None),
        P("replica", "dp", None),
        P("replica", "dp", None),
        P("replica", "dp"),
        P("replica"),
    )
    out_specs = (
        P(("dp", "replica"), None),
        P(("dp", "replica"), None),
        P(("dp", "replica"), None),
        P("replica", "dp", None),
    )
    return jax.shard_map(
        on_device, mesh=mesh, in_specs=in_specs, out_specs=out_specs, check_vma=False
    )
```

time: 904 us -> 92.9 us (0.10)
  waiting for transfers between devices: 777 us -> 0 us
  Pallas kernels: 0 us -> 86.9 us
  starting transfers between devices: 34.3 us -> 0 us
  blocking collectives: 32.3 us -> 0 us
  matrix products: 14.1 us -> 0 us
  between operations: 14.9 us -> 1.29 us
  other arithmetic: 11.5 us -> 1.46 us
    reduce_scatter x1 -> x0, waiting for transfers between devices: 636 us -> none  [on_device(): lax.psum_scatter(grad_terms.astype(jnp.bfloat16), 'dp', scatter_dimension...]
    all_gather x1 -> x0, waiting for transfers between devices: 140 us -> none  [on_device(): lax.all_gather(group_rows, 'dp', axis=0, tiled=True)]
    pallas_call x0 -> x1, Pallas kernels: none -> 86.9 us  [on_device(): pl.pallas_call(kernel, out_shape=(jax.ShapeDtypeStruct((16, 512), f32), j...]
    ppermute x9 -> x0, starting transfers between devices: 34.2 us -> none  [passed_along(): return lax.ppermute(block, axis, route)]
    all_gather x1 -> x0, blocking collectives: 32.3 us -> none  [on_device(): group_rows = lax.all_gather(rounded_rows, 'replica', axis=0, tiled=True)]
    dot_general x3 -> x0, matrix products: 14.1 us -> none  [the longest x1 5.41 us: prefill(): jnp.einsum('qhgd,khd->hgqk', query_heads, all_keys, preferred_element_typ...]
  transfers between devices with their start and end apart: 11 -> 0, of which waited for: 2 -> 0; matrix products, arithmetic and copies ran while one was open for 2% -> 0% of each run, Pallas kernels for 0% -> 0%
where the time goes in v2:
time: 92.9 us; the launch traced here: 91.9 us
  Pallas kernels  86.9 us (94%)
  local copies, waits for them, and re-layouts  2.29 us (2%)
  other arithmetic  1.46 us (2%)
  between operations  1.29 us (1%)
    pallas_call x1, Pallas kernels, on_device(): pl.pallas_call(kernel, out_shape=(jax.ShapeDtypeStruct((16, 512), f32), j...  86.9 us
    unnamed x1, local copies, waits for them, and re-layouts  2.29 us

profile of v2, /device:TPU:1, one launch (start us, length us, event | category | flops | bytes accessed | tf_op | source)
XLA Modules:
  0.0 91.9 jit_solution(1803589348728017985)
XLA Ops:
  1.3 86.9 %shard_map.120 = (f32[16,512]{1,0:T(8,128)}, bf16[128,4096]{1,0:T(8,128)(2,1)}) custom-call(bf16[16,2,16,512]{3,2,1,0:T(8,128)(2,1)} %bitcast.8, f32[16,512]{1,0:T(8,128)} %master_in.1, f32[16,512]{1,0:T(8,128)} %first_in.1, f32[16,512]{1,0:T(8,128)} %second_in.1, bf16[128,4096]{1,0:T(8,128)(2,1)} %bitcast.6, bf16[128,512]{1,0:T(8,128)(2,1)} %bitcast.9, ...), custom_call_target="tpu_custom_call" | custom-call | tf_op jit(solution)/shard_map/pallas_call | solution.py:489
  88.2 1.5 %multiply_subtract_fusion = (f32[16,512]{1,0:T(8,128)}, f32[16,512]{1,0:T(8,128)}, f32[16,512]{1,0:T(8,128)}) fusion(f32[16,512]{1,0:T(8,128)} %master_in.1, f32[16,512]{1,0:T(8,128)} %get-tuple-element.6, f32[16,512]{1,0:T(8,128)} %first_in.1, f32[16,512]{1,0:T(8,128)} %second_in.1), kind=kLoop, calls=%fused_computation.2 | loop fusion | flops 122880 | bytes 229376 | tf_op jit(solution)/shard_map/sub | solution.py:33
  89.6 2.3 %copy.15 = bf16[1,128,4096]{2,1,0:T(8,128)(2,1)} copy(bf16[1,128,4096]{2,1,0:T(8,128)(2,1)} %bitcast.7) | data formatting | bytes 2097152

commit v3 on v2

--- a/solution.py
+++ b/solution.py
@@ -19,8 +19,6 @@
 LOG2E = 1.4426950408889634
 UNROLL_S = 4
 UNROLL_M = 8
-UNROLL_W = 2
-LAST = 3
 
 
 def adam_update(grad_sum, master, moment_first, moment_second):
@@ -69,7 +67,7 @@
     z_terms,
     rounded,
     wbuf,
-    hbuf,
+    hset,
     kbuf,
     kpair,
     segsrc,
@@ -77,7 +75,8 @@
     bias,
     wts,
     tots,
-    vout,
+    parts,
+    gathered,
     vbuf,
     local_sem,
     send_sem,
@@ -88,6 +87,7 @@
     seg_sem,
     wz_sem,
     ring_sem,
+    part_sem,
     val_sem,
 ):
     i32 = jnp.int32
@@ -122,20 +122,33 @@
 
     def greet_z(d, carry):
         greet(device_at(x, y, mod(z + d, NZ), c))
-        greet(device_at(x, y, mod(z + d, NZ), 1 - c))
         return carry
 
     lax.fori_loop(1, NZ, greet_z, 0)
-    sibling = device_at(x, y, z, 1 - c)
     other_x = mod(x + 2, 4)
-    greet(sibling)
     for step in (1, 2, 3):
         greet(device_at(mod(x + step, 4), y, z, c))
-        greet(device_at(x, mod(y + step, 4), z, c))
     for offset in (1, -1, 4 * xh - 2):
         greet(device_at(other_x, y, mod(z + offset, NZ), c))
-    for offset in (0, 1, -1, 4 * xh - 2):
-        greet(device_at(other_x, y, mod(z + offset, NZ), 1 - c))
+
+    def member(k):
+        if k == 7:
+            return y, 1 - c
+        return mod(y + (2, 1, 3)[k // 2], 4), lax.rem(c + k % 2, i32(2))
+
+    members = [member(k) for k in (0, 1, 2, 3, 4, 5, 7)]
+    for my, mc in members:
+        greet(device_at(x, my, z, mc))
+    plane = 4 * c + y
+    for source in (plane, plane + 8):
+
+        @pl.when(source != z)
+        def _():
+            def greet_plane(n, carry):
+                greet(device_at(x, lax.div(n, i32(2)), source, lax.rem(n, i32(2))))
+                return carry
+
+            lax.fori_loop(0, 8, greet_plane, 0)
 
     def local(n, src, dst):
         copy = pltpu.make_async_copy(src, dst, local_sem.at[n])
@@ -153,9 +166,8 @@
         local(5, packed_in, packed_len),
         local(6, queries_in, queries),
         local(7, keys_in, kbuf.at[3]),
-        local(8, hidden, hbuf.at[c]),
-    )
-    pl.semaphore_wait(barrier, 30 + 1 + 6 + 3 + 4)
+    )
+    pl.semaphore_wait(barrier, 15 + 3 + 3 + 7 + 15)
 
     half_here = lax.div(z, i32(8))
     partner = device_at(other_x, y, z, c)
@@ -174,8 +186,25 @@
                 partner,
             )
 
-    hid_copy = send(hidden, hbuf.at[c], hid_sem.at[0], hid_sem.at[1], sibling)
+    next_z = device_at(x, y, mod(z + 1, NZ), c)
+    key_copies = [send(keys_in, kbuf.at[1], key_sem.at[5], key_sem.at[1], next_z)]
     pair_keys = send(keys_in, kpair, key_sem.at[4], key_sem.at[0], partner)
+
+    me = y * 2 + c
+    for my, mc in members:
+        for n in (0, 1):
+            cols = pl.ds(pl.multiple_of((4 * mc + my + 8 * n) * 512, 512), 512)
+            send(
+                hidden.at[:, cols],
+                hset.at[n, me],
+                hid_sem.at[0],
+                hid_sem.at[1],
+                device_at(x, my, z, mc),
+            )
+    for n in (0, 1):
+        cols = pl.ds(pl.multiple_of((plane + 8 * n) * 512, 512), 512)
+        pltpu.make_async_copy(hidden.at[:, cols], hset.at[n, me], hid_sem.at[1]).start()
+
     seg_local.wait()
     segsrc[...] = jnp.broadcast_to(segs[...], (8, 128))
     segbuf[3] = segsrc[...]
@@ -217,8 +246,6 @@
     for copy in state_local:
         copy.wait()
 
-    own_rows = pl.ds(pl.multiple_of(c * 16, 16), 16)
-
     def update(p):
         cols = slice(p * 256, (p + 1) * 256)
         wait_bytes(z_terms.at[p, pl.ds(0, 15)], z_sem.at[p])
@@ -226,124 +253,96 @@
         rows_new = adam_update(
             grad_sum, master[:, cols], moment_first[:, cols], moment_second[:, cols]
         )[3]
-        rounded[p, 0] = rows_new[:, :128]
-        rounded[p, 1] = rows_new[:, 128:]
-        mine = wbuf.at[p, z, xh, y, xl, own_rows]
-        arrived = wz_sem.at[p, z]
-        send(rounded.at[p, 1 - c], mine, send_sem.at[3], arrived, sibling)
-        for n in (0, 1):
-            for there in z_partners(n):
-                to, across = device_at(x, y, there, c), device_at(x, y, there, 1 - c)
-                send(rounded.at[p, c], mine, send_sem.at[2], arrived, to)
-                send(rounded.at[p, 1 - c], mine, send_sem.at[3], arrived, across)
-        wbuf[p, z, xh, y, xl, own_rows] = rounded[p, c]
+        rounded[p] = rows_new
+        side = lax.div(z, i32(8))
+        mine = wbuf.at[p, side, xh, y, xl, c]
+        ty, tc = lax.rem(z, i32(4)), lax.rem(lax.div(z, i32(4)), i32(2))
+
+        def send_z(d, carry):
+            send(
+                rounded.at[p],
+                mine,
+                send_sem.at[2],
+                wz_sem.at[p],
+                device_at(x, ty, mod(z + d, NZ), tc),
+            )
+            return carry
+
+        lax.fori_loop(1, NZ, send_z, 0)
+        here = (ty == y) & (tc == c)
+
+        @pl.when(here)
+        def _():
+            pltpu.make_async_copy(rounded.at[p], mine, wz_sem.at[p]).start()
+
+        @pl.when(jnp.logical_not(here))
+        def _():
+            send(rounded.at[p], mine, send_sem.at[3 + p], wz_sem.at[p], device_at(x, ty, z, tc))
+
         grad_out[:, cols] = grad_sum
 
-    steps = (1, 3, 2)
-    near_x = [device_at(mod(x + step, 4), y, z, c) for step in steps]
-    near_y = [device_at(x, mod(y + step, 4), z, c) for step in steps]
-
-    def x_split(value):
-        return lax.div(value, i32(2)), lax.rem(value, i32(2))
-
-    def four(n, colour):
-        return pl.ds(half_of(n) * 8 + 4 * colour, 4)
-
-    def two(n, colour, way):
-        return pl.ds(half_of(n) * 8 + 4 * colour + 2 * way, 2)
-
-    def column_at(colour, back):
-        if colour == 0:
-            fh, fl = x_split(mod(x + back, 4))
-            return fh, y, fl
-        return xh, mod(y + back, 4), xl
-
-    def line_at(p, zs, colour, back):
-        if colour == 0:
-            return wbuf.at[p, zs, :, mod(y + back, 4), :]
-        fh, fl = x_split(mod(x + back, 4))
-        return wbuf.at[p, zs, fh, :, fl]
-
-    def first_stage(r):
-        p, n = r // 2, r % 2
-        if n == 0:
-            wait_bytes(wbuf.at[p, z, xh, y, xl, pl.ds(0, 16)], wz_sem.at[p, z])
-        for zi in z_partners(n):
-            wait_bytes(wbuf.at[p, zi, xh, y, xl], wz_sem.at[p, zi])
-        for colour, near in ((0, near_x), (1, near_y)):
-            part = wbuf.at[p, four(n, colour), xh, y, xl]
-            for way in (2, 0, 1):
-                send(part, part, send_sem.at[4], ring_sem.at[0, r, colour, way], near[way])
-
-    def second_stage(r):
-        p, n = r // 2, r % 2
-        ways = (2, 0, 1) if r == LAST else (0, 1)
-        for colour, near in ((0, near_y), (1, near_x)):
-            for way in (0, 1, 2):
-                fh, fy, fl = column_at(colour, 4 - steps[way])
-                wait_bytes(
-                    wbuf.at[p, four(n, colour), fh, fy, fl], ring_sem.at[0, r, colour, way]
+    def column(p, back):
+        source = mod(x + back, 4)
+        return wbuf.at[p, :, lax.div(source, i32(2)), :, lax.rem(source, i32(2))]
+
+    def gather_x(p):
+        part = column(p, 0)
+        wait_bytes(part, wz_sem.at[p])
+        for n, step in enumerate((2, 1, 3)):
+            send(
+                part,
+                part,
+                send_sem.at[5],
+                ring_sem.at[p, n],
+                device_at(mod(x + step, 4), y, z, c),
+            )
+
+    def multiply(p):
+        for n, step in enumerate((2, 1, 3)):
+            wait_bytes(column(p, 4 - step), ring_sem.at[p, n])
+
+        def product(k, carry):
+            pair = pl.ds(k * 2, 2)
+            acc = jnp.dot(
+                hset[0, pair].reshape(256, 512),
+                wbuf[p, 0].reshape(512, 256),
+                preferred_element_type=jnp.float32,
+            )
+            acc = acc + jnp.dot(
+                hset[1, pair].reshape(256, 512),
+                wbuf[p, 1].reshape(512, 256),
+                preferred_element_type=jnp.float32,
+            )
+            parts[p, pair] = acc.astype(jnp.bfloat16).reshape(2, 128, 256)
+            return carry
+
+        lax.fori_loop(0, 4, product, 0)
+        for my, mc in members:
+            send(
+                parts.at[p, my * 2 + mc],
+                gathered.at[p, me],
+                send_sem.at[6],
+                part_sem.at[p],
+                device_at(x, my, z, mc),
+            )
+        gathered[p, me] = parts[p, me]
+
+    val_copies = ([], [])
+
+    def send_values(p):
+        wait_bytes(gathered.at[p, pl.ds(0, 7)], part_sem.at[p])
+        total = jnp.sum(gathered[p].astype(jnp.float32), axis=0)
+        vbuf[p, 3] = total.astype(jnp.bfloat16)
+        for o in (3, 2, 1):
+            val_copies[p].append(
+                send(
+                    vbuf.at[p, 3],
+                    vbuf.at[p, 3 - o],
+                    val_sem.at[p, 0, o],
+                    val_sem.at[p, 1, o],
+                    (mod(dp + o, 32), rep),
                 )
-            part = line_at(p, four(n, colour), colour, 0)
-            for way in ways:
-                send(part, part, send_sem.at[5], ring_sem.at[1, r, colour, way], near[way])
-
-    def second_forward(r):
-        p, n = r // 2, r % 2
-        for colour, near in ((0, near_y), (1, near_x)):
-            for way in (0, 1):
-                back = 4 - steps[way]
-                wait_bytes(
-                    line_at(p, four(n, colour), colour, back), ring_sem.at[1, r, colour, way]
-                )
-                part = line_at(p, two(n, colour, way), colour, back)
-                send(part, part, send_sem.at[6], ring_sem.at[2, r, colour, way], near[way])
-
-    def multiply(r, total):
-        p, n = r // 2, r % 2
-        for colour in (0, 1):
-            if r == LAST:
-                for way in (0, 1, 2):
-                    wait_bytes(
-                        line_at(p, four(n, colour), colour, 4 - steps[way]),
-                        ring_sem.at[1, r, colour, way],
-                    )
-            else:
-                for way in (0, 1):
-                    wait_bytes(
-                        line_at(p, two(n, colour, way), colour, 2),
-                        ring_sem.at[2, r, colour, way],
-                    )
-        g = half_of(n)
-
-        def add(i, acc):
-            zi = g * 8 + i
-            cols = pl.ds(pl.multiple_of(zi * 512, 512), 512)
-            return acc + jnp.dot(
-                hbuf[:, :, cols].reshape(256, 512),
-                wbuf[p, zi].reshape(512, 128),
-                preferred_element_type=jnp.float32,
-            )
-
-        return lax.fori_loop(0, 8, add, total, unroll=UNROLL_W)
-
-    val_copies = ([], [])
-
-    def send_values(p, total):
-        vout[p] = total.astype(jnp.bfloat16).reshape(2, 128, 128)
-        for o in (3, 2, 1, 0):
-            for other in (0, 1) if o else (1,):
-                core = lax.rem(c + other, i32(2))
-                val_copies[p].append(
-                    send(
-                        vout.at[p, core],
-                        vbuf.at[p, 3 - o, c],
-                        val_sem.at[p, 0, o, other],
-                        val_sem.at[p, 1, o, other],
-                        (mod(dp + o, 32), rep - c + core),
-                    )
-                )
-        vbuf[p, 3, c] = vout[p, c]
+            )
 
     def scores_of(head, carry):
         kv = lax.div(head, i32(8))
@@ -391,7 +390,7 @@
         pos = dp * 128 + lax.broadcasted_iota(i32, (128, HD), 0)
         live = pos < packed_len[0]
         for core in (0, 1):
-            v = vbuf[p, :, core].reshape(512, HD)
+            v = vbuf[p, :, :, core * HD : (core + 1) * HD].reshape(512, HD)
 
             def mix(j, carry):
                 head = (2 * p + core) * 8 + j
@@ -401,8 +400,6 @@
                 return carry
 
             lax.fori_loop(0, 8, mix, 0, unroll=UNROLL_M)
-
-    key_copies = []
 
     def far_keys():
         return pltpu.make_async_remote_copy(
@@ -416,56 +413,46 @@
 
     def send_keys():
         pair_keys.wait_recv()
-        next_z = device_at(x, y, mod(z + 1, NZ), c)
-
         @pl.when(xh == 0)
         def _():
             far_keys().start()
 
-        key_copies.append(send(keys_in, kbuf.at[1], key_sem.at[5], key_sem.at[1], next_z))
         key_copies.append(
             send(kpair, kbuf.at[2 - 2 * xh], key_sem.at[6], key_sem.at[2], next_z)
         )
 
-    zero = jnp.zeros((256, 128), jnp.float32)
     update(0)
     update(1)
     send_keys()
-    first_stage(0)
-    first_stage(1)
-    second_stage(0)
-    first_stage(2)
-    second_stage(1)
-    first_stage(3)
+    gather_x(0)
+    gather_x(1)
+    wait_bytes(hset, hid_sem.at[1])
+    multiply(0)
     for copy in late_local:
         copy.wait()
-    hid_copy.wait()
-    second_forward(0)
-    second_stage(2)
-    second_forward(1)
-    total = multiply(0, zero)
-    second_stage(3)
-    total = multiply(1, total)
-    send_values(0, total)
-    second_forward(2)
     make_bias()
     scores(0, 8)
-    total = multiply(2, zero)
-    total = multiply(3, total)
-    send_values(1, total)
+    multiply(1)
+    send_values(0)
     scores(8, 32)
+    send_values(1)
     for copy in val_copies[0]:
         copy.wait()
     mix_heads(0)
 
-    half = pl.ds(0, 16)
     wait_bytes(pair_terms, send_sem.at[0])
     wait_bytes(z_terms.at[:, pl.ds(0, 15)], send_sem.at[1])
-    wait_bytes(wbuf.at[:, pl.ds(0, 15), 0, 0, 0, half], send_sem.at[2])
-    wait_bytes(wbuf.at[:, :, 0, 0, 0, half], send_sem.at[3])
-    wait_bytes(wbuf.at[0, pl.ds(0, 6)], send_sem.at[4])
-    wait_bytes(wbuf.at[:, pl.ds(0, 9)], send_sem.at[5])
-    wait_bytes(wbuf.at[0, pl.ds(0, 6)], send_sem.at[6])
+    wait_bytes(z_terms.at[:, pl.ds(0, 15)], send_sem.at[2])
+    here = (lax.rem(z, i32(4)) == y) & (lax.rem(lax.div(z, i32(4)), i32(2)) == c)
+
+    @pl.when(jnp.logical_not(here))
+    def _():
+        wait_bytes(rounded.at[0], send_sem.at[3])
+        wait_bytes(rounded.at[1], send_sem.at[4])
+
+    wait_bytes(wbuf.at[:, :, :, pl.ds(0, 3)], send_sem.at[5])
+    wait_bytes(parts.at[:, pl.ds(0, 7)], send_sem.at[6])
+    wait_bytes(hset.at[:, pl.ds(0, 7)], hid_sem.at[0])
     for copy in val_copies[1]:
         copy.wait()
     mix_heads(1)
@@ -505,9 +492,9 @@
             pltpu.VMEM((2, NZ, 16, 256), bf16),
             pltpu.VMEM((2, NZ, 16, 256), bf16),
             pltpu.VMEM((2, NZ, 16, 256), bf16),
-            pltpu.VMEM((2, 2, 16, 128), bf16),
-            pltpu.VMEM((2, NZ, 2, 4, 2, 32, 128), bf16),
-            pltpu.VMEM((2, 128, 8192), bf16),
+            pltpu.VMEM((2, 16, 256), bf16),
+            pltpu.VMEM((2, 2, 2, 4, 2, 2, 16, 256), bf16),
+            pltpu.VMEM((2, 8, 128, 512), bf16),
             pltpu.VMEM((4, 128, 512), bf16),
             pltpu.VMEM((128, 512), bf16),
             pltpu.VMEM((8, 128), jnp.int32),
@@ -515,18 +502,20 @@
             pltpu.VMEM((128, 512), f32),
             pltpu.VMEM((32, 128, 512), bf16),
             pltpu.VMEM((32, 128, HD), f32),
-            pltpu.VMEM((2, 2, 128, 128), bf16),
-            pltpu.VMEM((2, 4, 2, 128, 128), bf16),
-            dma((9,)),
+            pltpu.VMEM((2, 8, 128, 256), bf16),
+            pltpu.VMEM((2, 8, 128, 256), bf16),
+            pltpu.VMEM((2, 4, 128, 256), bf16),
+            dma((8,)),
             dma((8,)),
             dma((2, 2)),
             dma((2,)),
             dma((2,)),
             dma((8,)),
             dma((6,)),
-            dma((2, NZ)),
-            dma((3, 4, 2, 3)),
-            dma((2, 2, 4, 2)),
+            dma((2,)),
+            dma((2, 3)),
+            dma((2,)),
+            dma((2, 2, 4)),
         ],
         compiler_params=pltpu.CompilerParams(
             collective_id=0, has_side_effects=True, vmem_limit_bytes=64 << 20

time: 92.9 us -> 85.3 us (0.918)
  Pallas kernels: 86.9 us -> 80 us
    pallas_call x1, Pallas kernels: 86.9 us -> 80 us  [on_device(): pl.pallas_call(kernel, out_shape=(jax.ShapeDtypeStruct((16, 512), f32), j...]
where the time goes in v3:
time: 85.3 us; the launch traced here: 85.1 us
  Pallas kernels  80 us (94%)
  local copies, waits for them, and re-layouts  2.29 us (3%)
  other arithmetic  1.46 us (2%)
  between operations  1.29 us (2%)
    pallas_call x1, Pallas kernels, on_device(): pl.pallas_call(kernel, out_shape=(jax.ShapeDtypeStruct((16, 512), f32), j...  80 us
    unnamed x1, local copies, waits for them, and re-layouts  2.29 us

profile of v3, /device:TPU:1, one launch (start us, length us, event | category | flops | bytes accessed | tf_op | source)
XLA Modules:
  0.0 85.1 jit_solution(15495249892000521722)
XLA Ops:
  1.3 80.0 %shard_map.120 = (f32[16,512]{1,0:T(8,128)}, bf16[128,4096]{1,0:T(8,128)(2,1)}) custom-call(bf16[16,2,16,512]{3,2,1,0:T(8,128)(2,1)} %bitcast.8, f32[16,512]{1,0:T(8,128)} %master_in.1, f32[16,512]{1,0:T(8,128)} %first_in.1, f32[16,512]{1,0:T(8,128)} %second_in.1, bf16[128,4096]{1,0:T(8,128)(2,1)} %bitcast.6, bf16[128,512]{1,0:T(8,128)(2,1)} %bitcast.9, ...), custom_call_target="tpu_custom_call" | custom-call | tf_op jit(solution)/shard_map/pallas_call | solution.py:476
  81.3 1.5 %multiply_subtract_fusion = (f32[16,512]{1,0:T(8,128)}, f32[16,512]{1,0:T(8,128)}, f32[16,512]{1,0:T(8,128)}) fusion(f32[16,512]{1,0:T(8,128)} %master_in.1, f32[16,512]{1,0:T(8,128)} %get-tuple-element.6, f32[16,512]{1,0:T(8,128)} %first_in.1, f32[16,512]{1,0:T(8,128)} %second_in.1), kind=kLoop, calls=%fused_computation.2 | loop fusion | flops 122880 | bytes 229376 | tf_op jit(solution)/shard_map/sub | solution.py:31
  82.8 2.3 %copy.15 = bf16[1,128,4096]{2,1,0:T(8,128)(2,1)} copy(bf16[1,128,4096]{2,1,0:T(8,128)(2,1)} %bitcast.7) | data formatting | bytes 2097152

commit v4 on v3

--- a/solution.py
+++ b/solution.py
@@ -253,93 +253,99 @@
         rows_new = adam_update(
             grad_sum, master[:, cols], moment_first[:, cols], moment_second[:, cols]
         )[3]
-        rounded[p] = rows_new
-        side = lax.div(z, i32(8))
-        mine = wbuf.at[p, side, xh, y, xl, c]
         ty, tc = lax.rem(z, i32(4)), lax.rem(lax.div(z, i32(4)), i32(2))
-
-        def send_z(d, carry):
-            send(
-                rounded.at[p],
-                mine,
-                send_sem.at[2],
-                wz_sem.at[p],
-                device_at(x, ty, mod(z + d, NZ), tc),
-            )
-            return carry
-
-        lax.fori_loop(1, NZ, send_z, 0)
         here = (ty == y) & (tc == c)
-
-        @pl.when(here)
-        def _():
-            pltpu.make_async_copy(rounded.at[p], mine, wz_sem.at[p]).start()
-
-        @pl.when(jnp.logical_not(here))
-        def _():
-            send(rounded.at[p], mine, send_sem.at[3 + p], wz_sem.at[p], device_at(x, ty, z, tc))
+        for q in (2 * p, 2 * p + 1):
+            rounded[q] = rows_new[:, (q % 2) * HD : (q % 2 + 1) * HD]
+            mine = wbuf.at[q, lax.div(z, i32(8)), xh, y, xl, c]
+
+            def send_z(d, carry):
+                send(
+                    rounded.at[q],
+                    mine,
+                    send_sem.at[2],
+                    wz_sem.at[q],
+                    device_at(x, ty, mod(z + d, NZ), tc),
+                )
+                return carry
+
+            lax.fori_loop(1, NZ, send_z, 0)
+
+            @pl.when(here)
+            def _():
+                pltpu.make_async_copy(rounded.at[q], mine, wz_sem.at[q]).start()
+
+            @pl.when(jnp.logical_not(here))
+            def _():
+                send(
+                    rounded.at[q],
+                    mine,
+                    send_sem.at[8 + q],
+                    wz_sem.at[q],
+                    device_at(x, ty, z, tc),
+                )
 
         grad_out[:, cols] = grad_sum
 
-    def column(p, back):
+    def column(q, back):
         source = mod(x + back, 4)
-        return wbuf.at[p, :, lax.div(source, i32(2)), :, lax.rem(source, i32(2))]
-
-    def gather_x(p):
-        part = column(p, 0)
-        wait_bytes(part, wz_sem.at[p])
+        return wbuf.at[q, :, lax.div(source, i32(2)), :, lax.rem(source, i32(2))]
+
+    def gather_x(q):
+        part = column(q, 0)
+        wait_bytes(part, wz_sem.at[q])
         for n, step in enumerate((2, 1, 3)):
             send(
                 part,
                 part,
                 send_sem.at[5],
-                ring_sem.at[p, n],
+                ring_sem.at[q, n],
                 device_at(mod(x + step, 4), y, z, c),
             )
 
-    def multiply(p):
+    def multiply(q):
         for n, step in enumerate((2, 1, 3)):
-            wait_bytes(column(p, 4 - step), ring_sem.at[p, n])
+            wait_bytes(column(q, 4 - step), ring_sem.at[q, n])
 
         def product(k, carry):
             pair = pl.ds(k * 2, 2)
             acc = jnp.dot(
                 hset[0, pair].reshape(256, 512),
-                wbuf[p, 0].reshape(512, 256),
+                wbuf[q, 0].reshape(512, HD),
                 preferred_element_type=jnp.float32,
             )
             acc = acc + jnp.dot(
                 hset[1, pair].reshape(256, 512),
-                wbuf[p, 1].reshape(512, 256),
+                wbuf[q, 1].reshape(512, HD),
                 preferred_element_type=jnp.float32,
             )
-            parts[p, pair] = acc.astype(jnp.bfloat16).reshape(2, 128, 256)
+            parts[q, pair] = acc.astype(jnp.bfloat16).reshape(2, 128, HD)
             return carry
 
-        lax.fori_loop(0, 4, product, 0)
+        lax.fori_loop(0, 4, product, 0, unroll=2)
         for my, mc in members:
             send(
-                parts.at[p, my * 2 + mc],
-                gathered.at[p, me],
+                parts.at[q, my * 2 + mc],
+                gathered.at[q, me],
                 send_sem.at[6],
-                part_sem.at[p],
+                part_sem.at[q],
                 device_at(x, my, z, mc),
             )
-        gathered[p, me] = parts[p, me]
-
-    val_copies = ([], [])
-
-    def send_values(p):
-        wait_bytes(gathered.at[p, pl.ds(0, 7)], part_sem.at[p])
-        total = jnp.sum(gathered[p].astype(jnp.float32), axis=0)
-        vbuf[p, 3] = total.astype(jnp.bfloat16)
+        gathered[q, me] = parts[q, me]
+
+    val_copies = ([], [], [], [])
+
+    def send_values(q):
+        wait_bytes(gathered.at[q, pl.ds(0, 7)], part_sem.at[q])
+        total = jnp.sum(gathered[q].astype(jnp.float32), axis=0)
+        vbuf[q, 3] = total.astype(jnp.bfloat16)
         for o in (3, 2, 1):
-            val_copies[p].append(
+            val_copies[q].append(
                 send(
-                    vbuf.at[p, 3],
-                    vbuf.at[p, 3 - o],
-                    val_sem.at[p, 0, o],
-                    val_sem.at[p, 1, o],
+                    vbuf.at[q, 3],
+                    vbuf.at[q, 3 - o],
+                    val_sem.at[q, 0, o],
+                    val_sem.at[q, 1, o],
                     (mod(dp + o, 32), rep),
                 )
             )
@@ -362,8 +368,10 @@
         lax.fori_loop(first, last, scores_of, 0, unroll=UNROLL_S)
 
     def make_bias():
-        for copy in seg_copies + key_copies:
+        for copy in seg_copies:
             copy.wait()
+        key_copies[0].wait()
+        key_copies[1].wait_send()
         pair_keys.wait_send()
 
         @pl.when(xh == 0)
@@ -386,59 +394,70 @@
                 allowed = same & (jnp.broadcast_to(dp, (128, 128)) >= o)
             bias[:, slot * 128 : (slot + 1) * 128] = jnp.where(allowed, 0.0, -1e30)
 
-    def mix_heads(p):
+    def mix_heads(q):
+        for copy in val_copies[q]:
+            copy.wait()
         pos = dp * 128 + lax.broadcasted_iota(i32, (128, HD), 0)
         live = pos < packed_len[0]
-        for core in (0, 1):
-            v = vbuf[p, :, :, core * HD : (core + 1) * HD].reshape(512, HD)
-
-            def mix(j, carry):
-                head = (2 * p + core) * 8 + j
-                out = jnp.dot(wts[head], v, preferred_element_type=jnp.float32)
-                out = jnp.where(live, out / tots[head], 0.0).astype(jnp.bfloat16)
-                attended[:, pl.ds(pl.multiple_of(head * HD, HD), HD)] = out
-                return carry
-
-            lax.fori_loop(0, 8, mix, 0, unroll=UNROLL_M)
+        v = vbuf[q].reshape(512, HD)
+
+        def mix(j, carry):
+            head = q * 8 + j
+            out = jnp.dot(wts[head], v, preferred_element_type=jnp.float32)
+            out = jnp.where(live, out / tots[head], 0.0).astype(jnp.bfloat16)
+            attended[:, pl.ds(pl.multiple_of(head * HD, HD), HD)] = out
+            return carry
+
+        lax.fori_loop(0, 8, mix, 0, unroll=UNROLL_M)
 
     def far_keys():
         return pltpu.make_async_remote_copy(
-            src_ref=kpair,
+            src_ref=kbuf.at[2],
             dst_ref=kbuf.at[0],
             send_sem=key_sem.at[7],
             recv_sem=key_sem.at[3],
-            device_id=device_at(x, y, mod(z + 2, NZ), c),
+            device_id=next_z,
             device_id_type=MESH,
         )
 
     def send_keys():
         pair_keys.wait_recv()
+        key_copies.append(
+            send(kpair, kbuf.at[2 - 2 * xh], key_sem.at[6], key_sem.at[2], next_z)
+        )
+
+    def forward_keys():
+        key_copies[1].wait_recv()
+
         @pl.when(xh == 0)
         def _():
             far_keys().start()
 
-        key_copies.append(
-            send(kpair, kbuf.at[2 - 2 * xh], key_sem.at[6], key_sem.at[2], next_z)
-        )
-
     update(0)
     update(1)
-    send_keys()
     gather_x(0)
     gather_x(1)
+    gather_x(2)
+    send_keys()
     wait_bytes(hset, hid_sem.at[1])
     multiply(0)
+    gather_x(3)
+    multiply(1)
+    send_values(0)
+    multiply(2)
+    send_values(1)
+    forward_keys()
+    multiply(3)
+    send_values(2)
     for copy in late_local:
         copy.wait()
     make_bias()
     scores(0, 8)
-    multiply(1)
-    send_values(0)
+    send_values(3)
     scores(8, 32)
-    send_values(1)
-    for copy in val_copies[0]:
-        copy.wait()
     mix_heads(0)
+    mix_heads(1)
+    mix_heads(2)
 
     wait_bytes(pair_terms, send_sem.at[0])
     wait_bytes(z_terms.at[:, pl.ds(0, 15)], send_sem.at[1])
@@ -447,15 +466,13 @@
 
     @pl.when(jnp.logical_not(here))
     def _():
-        wait_bytes(rounded.at[0], send_sem.at[3])
-        wait_bytes(rounded.at[1], send_sem.at[4])
+        for q in range(4):
+            wait_bytes(rounded.at[q], send_sem.at[8 + q])
 
     wait_bytes(wbuf.at[:, :, :, pl.ds(0, 3)], send_sem.at[5])
     wait_bytes(parts.at[:, pl.ds(0, 7)], send_sem.at[6])
     wait_bytes(hset.at[:, pl.ds(0, 7)], hid_sem.at[0])
-    for copy in val_copies[1]:
-        copy.wait()
-    mix_heads(1)
+    mix_heads(3)
 
 
 def on_device(
@@ -492,8 +509,8 @@
             pltpu.VMEM((2, NZ, 16, 256), bf16),
             pltpu.VMEM((2, NZ, 16, 256), bf16),
             pltpu.VMEM((2, NZ, 16, 256), bf16),
-            pltpu.VMEM((2, 16, 256), bf16),
-            pltpu.VMEM((2, 2, 2, 4, 2, 2, 16, 256), bf16),
+            pltpu.VMEM((4, 16, HD), bf16),
+            pltpu.VMEM((4, 2, 2, 4, 2, 2, 16, HD), bf16),
             pltpu.VMEM((2, 8, 128, 512), bf16),
             pltpu.VMEM((4, 128, 512), bf16),
             pltpu.VMEM((128, 512), bf16),
@@ -502,20 +519,20 @@
             pltpu.VMEM((128, 512), f32),
             pltpu.VMEM((32, 128, 512), bf16),
             pltpu.VMEM((32, 128, HD), f32),
-            pltpu.VMEM((2, 8, 128, 256), bf16),
-            pltpu.VMEM((2, 8, 128, 256), bf16),
-            pltpu.VMEM((2, 4, 128, 256), bf16),
+            pltpu.VMEM((4, 8, 128, HD), bf16),
+            pltpu.VMEM((4, 8, 128, HD), bf16),
+            pltpu.VMEM((4, 4, 128, HD), bf16),
             dma((8,)),
-            dma((8,)),
+            dma((12,)),
             dma((2, 2)),
             dma((2,)),
             dma((2,)),
             dma((8,)),
             dma((6,)),
-            dma((2,)),
-            dma((2, 3)),
-            dma((2,)),
-            dma((2, 2, 4)),
+            dma((4,)),
+            dma((4, 3)),
+            dma((4,)),
+            dma((4, 2, 4)),
         ],
         compiler_params=pltpu.CompilerParams(
             collective_id=0, has_side_effects=True, vmem_limit_bytes=64 << 20

time: 85.3 us -> 79.8 us (0.936)
  Pallas kernels: 80 us -> 74.5 us
    pallas_call x1, Pallas kernels: 80 us -> 74.5 us  [on_device(): pl.pallas_call(kernel, out_shape=(jax.ShapeDtypeStruct((16, 512), f32), j...]
where the time goes in v4:
time: 79.8 us; the launch traced here: 79.6 us
  Pallas kernels  74.5 us (93%)
  local copies, waits for them, and re-layouts  2.29 us (3%)
  other arithmetic  1.46 us (2%)
  between operations  1.29 us (2%)
    pallas_call x1, Pallas kernels, on_device(): pl.pallas_call(kernel, out_shape=(jax.ShapeDtypeStruct((16, 512), f32), j...  74.5 us
    unnamed x1, local copies, waits for them, and re-layouts  2.29 us

profile of v4, /device:TPU:1, one launch (start us, length us, event | category | flops | bytes accessed | tf_op | source)
XLA Modules:
  0.0 79.6 jit_solution(12179911756950514811)
XLA Ops:
  1.3 74.5 %shard_map.120 = (f32[16,512]{1,0:T(8,128)}, bf16[128,4096]{1,0:T(8,128)(2,1)}) custom-call(bf16[16,2,16,512]{3,2,1,0:T(8,128)(2,1)} %bitcast.8, f32[16,512]{1,0:T(8,128)} %master_in.1, f32[16,512]{1,0:T(8,128)} %first_in.1, f32[16,512]{1,0:T(8,128)} %second_in.1, bf16[128,4096]{1,0:T(8,128)(2,1)} %bitcast.6, bf16[128,512]{1,0:T(8,128)(2,1)} %bitcast.9, ...), custom_call_target="tpu_custom_call" | custom-call | tf_op jit(solution)/shard_map/pallas_call | solution.py:493
  75.8 1.5 %multiply_subtract_fusion = (f32[16,512]{1,0:T(8,128)}, f32[16,512]{1,0:T(8,128)}, f32[16,512]{1,0:T(8,128)}) fusion(f32[16,512]{1,0:T(8,128)} %master_in.1, f32[16,512]{1,0:T(8,128)} %get-tuple-element.6, f32[16,512]{1,0:T(8,128)} %first_in.1, f32[16,512]{1,0:T(8,128)} %second_in.1), kind=kLoop, calls=%fused_computation.2 | loop fusion | flops 122880 | bytes 229376 | tf_op jit(solution)/shard_map/sub | solution.py:31
  77.3 2.3 %copy.15 = bf16[1,128,4096]{2,1,0:T(8,128)(2,1)} copy(bf16[1,128,4096]{2,1,0:T(8,128)(2,1)} %bitcast.7) | data formatting | bytes 2097152

commit v5 on v4

--- a/solution.py
+++ b/solution.py
@@ -437,17 +437,17 @@
     update(1)
     gather_x(0)
     gather_x(1)
+    send_keys()
     gather_x(2)
-    send_keys()
     wait_bytes(hset, hid_sem.at[1])
     multiply(0)
     gather_x(3)
+    forward_keys()
     multiply(1)
+    multiply(2)
     send_values(0)
-    multiply(2)
+    multiply(3)
     send_values(1)
-    forward_keys()
-    multiply(3)
     send_values(2)
     for copy in late_local:
         copy.wait()
@@ -493,8 +493,8 @@
     grad_sum, attended = pl.pallas_call(
         kernel,
         out_shape=(
-            jax.ShapeDtypeStruct((16, 512), f32),
-            jax.ShapeDtypeStruct((128, 4096), bf16),
+            pltpu.VMEM((16, 512), f32),
+            pltpu.VMEM((128, 4096), bf16),
         ),
         in_specs=[hbm] * 9,
         out_specs=(vmem, vmem),
@@ -535,7 +535,7 @@
             dma((4, 2, 4)),
         ],
         compiler_params=pltpu.CompilerParams(
-            collective_id=0, has_side_effects=True, vmem_limit_bytes=64 << 20
+            collective_id=0, has_side_effects=True, vmem_limit_bytes=62 << 20
         ),
     )(
         grad_parts.reshape(NZ, 2, 16, 512),

time: 79.8 us -> 75.1 us (0.941)
  Pallas kernels: 74.5 us -> 71.4 us
  local copies, waits for them, and re-layouts: 2.29 us -> 0.99 us
  other arithmetic: 1.46 us -> 0.65 us
    pallas_call x1, Pallas kernels: 74.5 us -> 71.4 us  [on_device(): pl.pallas_call(kernel, out_shape=(pltpu.VMEM((16, 512), f32), pltpu.VMEM(...]
    unnamed x1 -> x7, local copies, waits for them, and re-layouts: 2.29 us -> 0.99 us
    sub x1, other arithmetic: 1.46 us -> 0.65 us  [adam_update(): master_new = master - learn_rate * step_dir]
where the time goes in v5:
time: 75.1 us; the launch traced here: 74.4 us
  Pallas kernels  71.4 us (95%)
  between operations  1.31 us (2%)
  local copies, waits for them, and re-layouts  0.99 us (1%)
    pallas_call x1, Pallas kernels, on_device(): pl.pallas_call(kernel, out_shape=(pltpu.VMEM((16, 512), f32), pltpu.VMEM(...  71.4 us

profile of v5, /device:TPU:1, one launch (start us, length us, event | category | flops | bytes accessed | tf_op | source)
XLA Modules:
  0.0 74.4 jit_solution(1096973154477771911)
XLA Ops:
  1.3 0.0 copy-start
  1.3 0.0 copy-start.1
  1.3 0.0 copy-start.2
  1.3 71.4 %shard_map.120 = (f32[16,512]{1,0:T(8,128)S(1)}, bf16[128,4096]{1,0:T(8,128)(2,1)S(1)}) custom-call(bf16[16,2,16,512]{3,2,1,0:T(8,128)(2,1)} %bitcast.8, f32[16,512]{1,0:T(8,128)} %master_in.1, f32[16,512]{1,0:T(8,128)} %first_in.1, f32[16,512]{1,0:T(8,128)} %second_in.1, bf16[128,4096]{1,0:T(8,128)(2,1)} %bitcast.7, bf16[128,512]{1,0:T(8,128)(2,1)} %bitcast.9, ...), custom_call_target="tpu_custom_call" | custom-call | tf_op jit(solution)/shard_map/pallas_call | solution.py:493
  72.7 1.0 %copy.14 = bf16[1,128,4096]{2,1,0:T(8,128)(2,1)} copy(bf16[1,128,4096]{2,1,0:T(8,128)(2,1)S(1)} %bitcast.5) | data formatting | bytes 2097152
  73.7 0.0 copy-done
  73.7 0.0 copy-done.1
  73.7 0.0 copy-done.2
  73.7 0.7 multiply_subtract_fusion
Async XLA Ops:
  1.3 72.4 %copy-start = (f32[16,512]{1,0:T(8,128)S(1)}, f32[16,512]{1,0:T(8,128)}, u32[]{:S(2)}) copy-start(f32[16,512]{1,0:T(8,128)} %master_in.1) | copy-start | bytes 98308
  1.3 72.4 %copy-start.1 = (f32[16,512]{1,0:T(8,128)S(1)}, f32[16,512]{1,0:T(8,128)}, u32[]{:S(2)}) copy-start(f32[16,512]{1,0:T(8,128)} %first_in.1) | copy-start | bytes 98308
  1.3 72.4 %copy-start.2 = (f32[16,512]{1,0:T(8,128)S(1)}, f32[16,512]{1,0:T(8,128)}, u32[]{:S(2)}) copy-start(f32[16,512]{1,0:T(8,128)} %second_in.1) | copy-start | bytes 98308
